TPU v7x, 128 devices: a whole 4x4x4 slice. The times are simulated.
128 devices in a mesh: replica: 16 (over z, y), tensor: 8 (over x, core).
Axes of the slice: x: 4, y: 4, z: 4, core: 2. Of those that a mesh axis runs over, the one named last changes fastest.
Arguments:
- attended: bfloat16 [16384, 8192], P('replica', 'tensor'), may hold values from -6 to 6
- out_weight: bfloat16 [8192, 8192], P('tensor'), may hold values from -0.09375 to 0.09375
- shrink_weight: bfloat16 [192, 64, 8192], P('replica', None, 'tensor'), may hold values from -0.0625 to 0.0625
- expand_weight: bfloat16 [192, 64, 8192], P('replica', None, 'tensor'), may hold values from -0.75 to 0.75
- block_adapter: int32 [128], P('replica'), may hold values from 0 to 191, as said below
- block_fill: int32 [128], P('replica'), may hold values from 1 to 128
Outputs:
- projected: bfloat16 [16384, 8192], P('replica', 'tensor')
Inputs may be any that keep to these rules, and one draw needn't show every extreme that they name: `block_adapter`: the owner of adapter j is replica j // 12. Among the 8 blocks of one replica, at most 1 have adapters of one owner; one owner gets exactly 1 block from every replica.
All inputs are finite; a program needn't handle non-finite values.
Results may differ from a plain program's by a relative error of at most 0.02.
Values may be sent and summed in bfloat16 or wider, within the bound.
No kernel may reach another device: no remote copies, remote signals or barrier semaphores. Data moves between devices by JAX's collectives and lax.ppermute only.
A program may use at most 128 MiB of HBM per device.

v0:
```python
import jax
import jax.numpy as jnp
from jax import lax
from jax.sharding import PartitionSpec as P


def slot_layout(block_ids, per_owner, capacity):
    block_owner = block_ids // per_owner
    local_ids = block_ids - block_owner * per_owner
    positions = jnp.arange(block_ids.shape[-1])
    earlier_same = (block_owner[..., None, :] == block_owner[..., :, None]) & (
        positions[None, :] < positions[:, None]
    )
    slot_rank = jnp.sum(earlier_same.astype(jnp.int32), axis=-1)
    return (block_owner * capacity + slot_rank, local_ids)


def local(attended, out_weight, shrink_weight, expand_weight, block_adapter, block_fill):
    tok_rows, feature_piece = attended.shape
    block_count = block_adapter.shape[0]
    block_rows = tok_rows // block_count
    owner_count = lax.axis_size("replica")
    capacity = max(1, (2 * block_count + owner_count - 1) // owner_count)
    per_owner = shrink_weight.shape[0]
    slot_count = owner_count * capacity
    slot_index, local_ids = slot_layout(block_adapter, per_owner, capacity)
    block_table = lax.all_gather(block_adapter, "replica", axis=0, tiled=True).reshape(
        owner_count, block_count
    )
    all_slots, all_local = slot_layout(block_table, per_owner, capacity)
    wanted_slot = lax.axis_index("replica") * capacity + jnp.arange(capacity)
    served_hit = all_slots[:, None, :] == wanted_slot[None, :, None]
    served_ids = jnp.sum(jnp.where(served_hit, all_local[:, None, :], 0), axis=-1)
    row_blocks = attended.reshape(block_count, block_rows, feature_piece)
    slot_match = jnp.arange(slot_count)[:, None] == slot_index[None, :]
    slot_source = jnp.sum(jnp.where(slot_match, jnp.arange(block_count)[None, :], 0), axis=1)
    slot_filled = jnp.any(slot_match, axis=1)
    outgoing = jnp.where(slot_filled[:, None, None], row_blocks[slot_source], 0)
    outgoing = outgoing.reshape(owner_count, capacity, block_rows, feature_piece)
    arrived = lax.all_to_all(outgoing, "replica", split_axis=0, concat_axis=0, tiled=True)
    partial_low = jnp.einsum(
        "scbp,scrp->scrb", arrived, shrink_weight[served_ids], preferred_element_type=jnp.float32
    )
    low_rank = lax.psum(partial_low.astype(jnp.bfloat16), "tensor")
    delta_slots = jnp.einsum(
        "scrb,scrp->scbp", low_rank, expand_weight[served_ids], preferred_element_type=jnp.float32
    ).astype(jnp.bfloat16)
    returned = lax.all_to_all(delta_slots, "replica", split_axis=0, concat_axis=0, tiled=True)
    delta_rows = returned.reshape(slot_count, block_rows, feature_piece)[slot_index]
    partial_out = jnp.dot(attended, out_weight, preferred_element_type=jnp.float32)
    base_out = lax.psum_scatter(
        partial_out.astype(jnp.bfloat16), "tensor", scatter_dimension=1, tiled=True
    ).astype(jnp.float32)
    combined = base_out.reshape(block_count, block_rows, feature_piece) + delta_rows.astype(
        jnp.float32
    )
    live_rows = jnp.arange(block_rows)[None, :] < block_fill[:, None]
    projected = jnp.where(live_rows[:, :, None], combined, 0.0).astype(jnp.bfloat16)
    return projected.reshape(tok_rows, feature_piece)


def solution(mesh):
    in_specs = (
        P("replica", "tensor"),
        P("tensor", None),
        P("replica", None, "tensor"),
        P("replica", None, "tensor"),
        P("replica"),
        P("replica"),
    )
    out_specs = P("replica", "tensor")
    return jax.shard_map(local, mesh=mesh, in_specs=in_specs, out_specs=out_specs, check_vma=False)
```

profile of v0, /device:TPU:14, one launch (start us, length us, event | category | flops | bytes accessed | tf_op | source)
XLA Modules:
  0.0 264.8 jit_solution(30264454527374163)
XLA Ops:
  6.5 0.8 and_select_fusion
  7.4 0.2 convert_reduce_fusion.1
  7.5 0.7 compare_select_fusion
  8.2 0.1 select_reduce_fusion
  8.3 0.1 fusion.7
  8.4 0.0 copy-done
  8.4 2.8 %gather_fusion.1 = bf16[16,128,1024]{2,1,0:T(8,128)(2,1)} fusion(bf16[8,128,1024]{2,1,0:T(8,128)(2,1)S(1)} %bitcast.32, s32[1024]{0:T(1024)S(1)} %pad_clamp_fusion.1), kind=kCustom, calls=%fused_computation.1 | custom fusion | bytes 8388672 | tf_op jit(solution)/shard_map/gather | solution.py:38
  11.2 4.5 %bitcast_select_fusion = bf16[16,1,128,1024]{3,2,1,0:T(8,128)(2,1)} fusion(bf16[16,128,1024]{2,1,0:T(8,128)(2,1)} %gather_fusion.1, pred[16]{0:T(512)(128)(4,1)S(1)} %fusion.7), kind=kLoop, calls=%fused_computation.10 | loop fusion | flops 2097152 | bytes 8388624 | tf_op jit(solution)/shard_map/jit(_where)/select_n | solution.py:38
  15.7 8.5 %all-to-all-start = ((bf16[16,1,128,1024]{3,2,1,0:T(8,128)(2,1)}), bf16[16,1,128,1024]{3,2,1,0:T(8,128)(2,1)}, u32[]{:S(2)}, u32[]{:S(2)}) async-start(bf16[16,1,128,1024]{3,2,1,0:T(8,128)(2,1)} %bitcast_select_fusion), calls=%async_computation.1 | async-start | bytes 8388608 | tf_op jit(solution)/shard_map/all_to_all | solution.py:40
  24.2 0.0 all-reduce.3.cloned.1.call-start
  24.3 0.6 dynamic-slice
  25.5 0.2 dynamic-update-slice
  25.8 68.0 %all-reduce = s32[128]{0:T(128)S(1)} all-reduce(s32[128]{0:T(128)S(1)} %dynamic-update-slice), channel_id=1, replica_groups=mesh['replica'=16,'tensor'=8] {'replica'}, use_global_device_ids=true, to_apply=%add | all-reduce | flops 128 | bytes 1024
  93.8 0.1 reshape.153
  93.9 0.1 copy.8
  94.0 0.1 convert_reduce_fusion
  94.2 3.4 %gather_fusion = bf16[16,64,1024]{2,1,0:T(8,128)(2,1)} fusion(bf16[12,64,1024]{2,1,0:T(8,128)(2,1)} %param.8, s32[1024]{0:T(1024)S(1)} %pad_clamp_fusion.2), kind=kCustom, calls=%fused_computation | custom fusion | bytes 4194368 | tf_op jit(solution)/shard_map/gather | solution.py:42
  97.6 0.0 all-to-all-done
  97.6 5.1 %fusion.4 = bf16[16,64,128]{2,1,0:T(8,128)(2,1)} fusion(bf16[16,64,1024]{2,1,0:T(8,128)(2,1)} %gather_fusion, bf16[16,1,128,1024]{3,2,1,0:T(8,128)(2,1)} %all-to-all-done), kind=kOutput, calls=%fused_computation.12 | convolution fusion | flops 268566528 | bytes 6553600 | tf_op jit(solution)/shard_map/scbp,scrp->scrb/dot_general | solution.py:41
  102.7 0.0 all-reduce.3.cloned.1.call-update
  102.7 0.0 reduce-scatter.2.cloned.1.call-start
  102.7 25.8 %convolution_convert_fusion = bf16[1024,8192]{1,0:T(8,128)(2,1)} fusion(bf16[1024,1024]{1,0:T(8,128)(2,1)S(1)} %copy-done, bf16[1024,8192]{1,0:T(8,128)(2,1)} %param.7), kind=kOutput, calls=%fused_computation.4 | convolution fusion | flops 17188257792 | bytes 35651584 | tf_op jit(solution)/shard_map/dot_general | solution.py:50
  128.5 0.0 reduce-scatter.2.cloned.1.call-update
  128.6 2.1 gather_fusion.2
  130.7 29.2 %all-reduce.3.cloned.1.call-done = bf16[16,64,128]{2,1,0:T(8,128)(2,1)} async-done(((bf16[16,64,128]{2,1,0:T(8,128)(2,1)}), bf16[16,64,128]{2,1,0:T(8,128)(2,1)}) %all-reduce.3.cloned.1.call-update) | async-done | bytes 262160 | tf_op jit(solution)/shard_map/psum | solution.py:44
  159.9 4.2 %convert_bitcast_fusion = bf16[16,1,128,1024]{3,2,1,0:T(8,128)(2,1)} fusion(bf16[16,64,128]{2,1,0:T(8,128)(2,1)} %all-reduce.3.cloned.1.call-done, bf16[16,64,1024]{2,1,0:T(8,128)(2,1)S(1)} %gather_fusion.2), kind=kOutput, calls=%fused_computation.11 | convolution fusion | flops 270532608 | bytes 6553600 | tf_op jit(solution)/shard_map/scrb,scrp->scbp/dot_general | solution.py:45
  164.1 7.6 %all-to-all-start.1 = ((bf16[16,1,128,1024]{3,2,1,0:T(8,128)(2,1)}), bf16[16,1,128,1024]{3,2,1,0:T(8,128)(2,1)}, u32[]{:S(2)}, u32[]{:S(2)}) async-start(bf16[16,1,128,1024]{3,2,1,0:T(8,128)(2,1)} %convert_bitcast_fusion), calls=%async_computation.2 | async-start | bytes 8388608 | tf_op jit(solution)/shard_map/all_to_all | solution.py:48
  171.7 0.1 fusion.8
  171.7 60.9 %all-to-all-done.1 = bf16[16,1,128,1024]{3,2,1,0:T(8,128)(2,1)} async-done(((bf16[16,1,128,1024]{3,2,1,0:T(8,128)(2,1)}), bf16[16,1,128,1024]{3,2,1,0:T(8,128)(2,1)}, u32[]{:S(2)}, u32[]{:S(2)}) %all-to-all-start.1) | async-done | bytes 4194336 | tf_op jit(solution)/shard_map/all_to_all | solution.py:48
  232.7 4.4 %gather_fusion.3 = bf16[8,128,1024]{2,1,0:T(8,128)(2,1)} fusion(bf16[16,128,1024]{2,1,0:T(8,128)(2,1)} %bitcast.11, s32[1024]{0:T(1024)S(1)} %pad_clamp_fusion), kind=kCustom, calls=%fused_computation.3 | custom fusion | bytes 4194336 | tf_op jit(solution)/shard_map/gather | solution.py:49
  237.1 16.6 %reduce-scatter.2.cloned.1.call-done = bf16[1024,1024]{1,0:T(8,128)(2,1)} async-done(((bf16[1024,8192]{1,0:T(8,128)(2,1)}), bf16[1024,1024]{1,0:T(8,128)(2,1)}) %reduce-scatter.2.cloned.1.call-update) | async-done | bytes 2097168 | tf_op jit(solution)/shard_map/reduce_scatter | solution.py:51
  253.7 4.2 %fusion.1 = bf16[1024,1024]{1,0:T(8,128)(2,1)} fusion(bf16[1024,1024]{1,0:T(8,128)(2,1)} %reduce-scatter.2.cloned.1.call-done, bf16[8,128,1024]{2,1,0:T(8,128)(2,1)} %gather_fusion.3, pred[1024]{0:T(1024)(128)(4,1)S(1)} %fusion.8), kind=kLoop, calls=%fused_computation.7 | loop fusion | flops 5242880 | bytes 6292480 | tf_op jit(solution)/shard_map/convert_element_type | solution.py:58
  (18 shorter events, 0.1 us)
Async XLA Ops:
  6.5 1.9 copy-start
  15.7 8.6 %copy-start.4 = (u32[128]{0:T(128)S(1)}, u32[128]{0:T(128)}, u32[]{:S(2)}) copy-start(u32[128]{0:T(128)} %constant.44) | copy-start | bytes 1540
  15.7 9.9 %copy-start.2 = (s32[8]{0:T(128)S(1)}, s32[8]{0:T(128)}, u32[]{:S(2)}) copy-start(s32[8]{0:T(128)} %param.10) | copy-start | bytes 100
  15.7 81.9 %all-to-all-start = ((bf16[16,1,128,1024]{3,2,1,0:T(8,128)(2,1)}), bf16[16,1,128,1024]{3,2,1,0:T(8,128)(2,1)}, u32[]{:S(2)}, u32[]{:S(2)}) async-start(bf16[16,1,128,1024]{3,2,1,0:T(8,128)(2,1)} %bitcast_select_fusion), calls=%async_computation.1 | async-start | bytes 8388608 | tf_op jit(solution)/shard_map/all_to_all | solution.py:40
  24.2 135.7 %all-reduce.3.cloned.1.call-start = ((), (), s32[]{:S(2)}) async-start(), calls=%async_computation.4 | async-start | bytes 524288 | tf_op jit(solution)/shard_map/psum | solution.py:44
  102.7 151.1 %reduce-scatter.2.cloned.1.call-start = ((), (), s32[]{:S(2)}) async-start(), calls=%async_computation.3 | async-start | bytes 18874368 | tf_op jit(solution)/shard_map/reduce_scatter | solution.py:51
  164.1 7.6 %copy-start.3 = (s32[8]{0:T(128)S(1)}, s32[8]{0:T(128)}, u32[]{:S(2)}) copy-start(s32[8]{0:T(128)} %param.11) | copy-start | bytes 100
  164.1 68.6 %all-to-all-start.1 = ((bf16[16,1,128,1024]{3,2,1,0:T(8,128)(2,1)}), bf16[16,1,128,1024]{3,2,1,0:T(8,128)(2,1)}, u32[]{:S(2)}, u32[]{:S(2)}) async-start(bf16[16,1,128,1024]{3,2,1,0:T(8,128)(2,1)} %convert_bitcast_fusion), calls=%async_computation.2 | async-start | bytes 8388608 | tf_op jit(solution)/shard_map/all_to_all | solution.py:48
  232.7 25.2 %copy-start.1 = (bf16[1024,1024]{1,0:T(8,128)(2,1)S(1)}, bf16[1024,1024]{1,0:T(8,128)(2,1)}, u32[]{:S(2)}) copy-start(bf16[1024,1024]{1,0:T(8,128)(2,1)} %param.6) | copy-start | bytes 6291460
Sparse Core Ops, SparseCore 0:
  102.8 57.0 all-reduce.2
  162.5 91.1 reduce-scatter.1
where the time goes:
time: 268 us; the launch traced here: 265 us
  waiting for transfers between devices  107 us (40%)
  blocking collectives  68 us (25%)
  matrix products  35.1 us (13%)
  starting transfers between devices  16.2 us (6%)
  between operations  14.1 us (5%)
  local copies, waits for them, and re-layouts  13.7 us (5%)
  other arithmetic  10.8 us (4%)
    unnamed x1, blocking collectives  68 us
    all_to_all x1, waiting for transfers between devices, local(): lax.all_to_all(delta_slots, 'replica', split_axis=0, concat_axis=0, tiled...  60.9 us
    psum x1, waiting for transfers between devices, local(): low_rank = lax.psum(partial_low.astype(jnp.bfloat16), 'tensor')  29.2 us
    dot_general x1, matrix products, local(): jnp.dot(attended, out_weight, preferred_element_type=jnp.float32)  25.8 us
    reduce_scatter x1, waiting for transfers between devices, local(): lax.psum_scatter(partial_out.astype(jnp.bfloat16), 'tensor', scatter_dime...  16.6 us
    all_to_all x1, starting transfers between devices, local(): lax.all_to_all(outgoing, 'replica', split_axis=0, concat_axis=0, tiled=True)  8.54 us
    all_to_all x1, starting transfers between devices, local(): lax.all_to_all(delta_slots, 'replica', split_axis=0, concat_axis=0, tiled...  7.56 us
  transfers between devices with their start and end apart: 4, of which 3 were waited for; matrix products, arithmetic and copies ran while one was open for 16% of the time, Pallas kernels for 0%

commit v1 on v0

v1 whole, which is shorter than its diff:
```python
import functools

import jax
import jax.numpy as jnp
from jax import lax
from jax.experimental import pallas as pl
from jax.experimental.pallas import tpu as pltpu
from jax.sharding import PartitionSpec as P

BN = 512
IDS = 1
COST = pl.CostEstimate(flops=10_000_000_000, bytes_accessed=10_000_000, transcendentals=0)


def any_spec():
    return pl.BlockSpec(memory_space=pl.ANY)


def in_hbm(a):
    return pltpu.with_memory_space_constraint(a, pltpu.HBM)


def params():
    return pltpu.CompilerParams(vmem_limit_bytes=20 * 1024 * 1024)


def choose(values, k):
    out = values[-1]
    for i in range(len(values) - 2, -1, -1):
        out = jnp.where(k == i, values[i], out) if values[i] is not out else out
    return out


def clamp(g, steps, k):
    return jnp.clip(g - k * steps, 0, steps - 1)


def tasks_kernel(tasks, steps, sched, a_ref, ap_ref, w_ref, *refs):
    n = len(tasks)
    others, adds, outs = refs[:n], refs[n:], refs[-n:]
    at = 0
    for k, count in enumerate(tasks):
        mine = adds[at:at + count]
        at += count

        @pl.when(pl.program_id(0) // steps == k)
        def _(k=k, mine=mine):
            acc = jnp.dot(a_ref[...], w_ref[...], preferred_element_type=jnp.float32)
            acc = acc + jnp.dot(ap_ref[...], others[k][...], preferred_element_type=jnp.float32)
            for add in mine:
                acc = acc + add[...].astype(jnp.float32)
            outs[k][...] = acc.astype(outs[k].dtype)


def matmuls(sched, att, att_other, weight, rows, tasks, deps=()):
    width = att.shape[1]
    depth = weight.shape[0]
    steps = width // BN

    def a_map(g, s):
        return (choose([t[1] // rows for t in tasks], g // steps), 0)

    def w_map(g, s):
        slot = choose([t[0] for t in tasks], g // steps)
        return (0, s[slot] * steps + g % steps)

    in_specs = [pl.BlockSpec((rows, width), a_map), pl.BlockSpec((rows, width), a_map), pl.BlockSpec((depth, BN), w_map)]
    operands = [att, att_other, weight]
    for k, task in enumerate(tasks):
        array, row = task[2]
        in_specs.append(pl.BlockSpec((depth, BN), lambda g, s, k=k, row=row: (row // depth, clamp(g, steps, k))))
        operands.append(array)
    for k, task in enumerate(tasks):
        for array, row in task[3]:
            in_specs.append(pl.BlockSpec((rows, BN), lambda g, s, k=k, row=row: (row // rows, clamp(g, steps, k))))
            operands.append(array)
    in_specs += [any_spec() for _ in deps]
    return pl.pallas_call(
        functools.partial(tasks_kernel, [len(t[3]) for t in tasks], steps),
        grid_spec=pltpu.PrefetchScalarGridSpec(
            num_scalar_prefetch=1,
            grid=(steps * len(tasks),),
            in_specs=in_specs,
            out_specs=[pl.BlockSpec((rows, BN), lambda g, s, k=k: (0, clamp(g, steps, k))) for k in range(len(tasks))],
        ),
        out_shape=[pltpu.HBM((rows, width), jnp.bfloat16) for _ in tasks],
        compiler_params=params(),
        cost_estimate=COST,
    )(sched, *[in_hbm(a) for a in operands], *[in_hbm(a) for a in deps])


def shrink_kernel(blocks, rows, adapters, a_ref, *refs):
    o_ref = refs[-1]
    for b in range(blocks):
        o_ref[b] = lax.dot_general(
            refs[b][0], a_ref[b * rows:(b + 1) * rows, :], (((1,), (1,)), ((), ())), preferred_element_type=jnp.float32
        ).astype(o_ref.dtype)


def shrink(adapters, att, slots, per_owner, deps=()):
    blocks = adapters.shape[0]
    rows = att.shape[0] // blocks
    _, rank, width = slots.shape
    in_specs = [pl.BlockSpec(att.shape, lambda g, ad: (0, 0))]
    for b in range(blocks):
        in_specs.append(pl.BlockSpec((1, rank, width), lambda g, ad, b=b: (ad[b] // per_owner, 0, 0)))
    in_specs += [any_spec() for _ in deps]
    return pl.pallas_call(
        functools.partial(shrink_kernel, blocks, rows),
        grid_spec=pltpu.PrefetchScalarGridSpec(
            num_scalar_prefetch=1,
            grid=(1,),
            in_specs=in_specs,
            out_specs=pl.BlockSpec((blocks, rank, rows), lambda g, ad: (0, 0, 0)),
        ),
        out_shape=jax.ShapeDtypeStruct((blocks, rank, rows), jnp.bfloat16),
        compiler_params=params(),
        cost_estimate=COST,
    )(adapters, in_hbm(att), *([in_hbm(slots)] * blocks), *[in_hbm(a) for a in deps])


def final_kernel(per, n_low, sched, adapters, fill, a_ref, ap_ref, w_ref, wp_ref, *refs):
    pairs, refs = refs[:4], refs[4:]
    lows, refs = refs[:n_low], refs[n_low:]
    expands, o_ref = refs[:2 * per], refs[-1]
    rows = a_ref.shape[0]
    block = rows // per
    for k in range(2):

        @pl.when(pl.program_id(0) == k)
        def _(k=k):
            base = jnp.dot(a_ref[...], w_ref[...], preferred_element_type=jnp.float32)
            base = base + jnp.dot(ap_ref[...], wp_ref[...], preferred_element_type=jnp.float32)
            for add in (pairs[2 * k], pairs[2 * k + 1]):
                base = base + add[...].astype(jnp.float32)
            for i in range(per):
                b = k * per + i
                low = lows[0][b].astype(jnp.float32)
                for other in lows[1:]:
                    low = low + other[b].astype(jnp.float32)
                delta = lax.dot_general(
                    low.astype(jnp.bfloat16), expands[b][0], (((0,), (0,)), ((), ())), preferred_element_type=jnp.float32
                ).astype(jnp.bfloat16)
                out = base[i * block:(i + 1) * block] + delta.astype(jnp.float32)
                live = lax.broadcasted_iota(jnp.int32, out.shape, 0) < fill[b]
                o_ref[i * block:(i + 1) * block, :] = jnp.where(live, out, 0.0).astype(o_ref.dtype)


def finish(sched, adapters, fill, att, att_other, weight, weight_other, pairs, lows, expand_slots, per_owner):
    blocks = adapters.shape[0]
    tokens, width = att.shape
    rows = tokens // 2
    steps = width // BN
    per = blocks // 2
    rank = expand_slots.shape[1]
    in_specs = [
        pl.BlockSpec((rows, width), lambda k, j, s, ad, fl: (k, 0)),
        pl.BlockSpec((rows, width), lambda k, j, s, ad, fl: (k, 0)),
        pl.BlockSpec((weight.shape[0], BN), lambda k, j, s, ad, fl: (0, s[0] * steps + j)),
        pl.BlockSpec((weight.shape[0], BN), lambda k, j, s, ad, fl: (0, j)),
    ]
    for k0 in range(2):
        for _ in range(2):
            in_specs.append(
                pl.BlockSpec((rows, BN), lambda k, j, s, ad, fl, k0=k0: (0, clamp(k * steps + j, steps, k0)))
            )
    for low in lows:
        in_specs.append(pl.BlockSpec(low.shape, lambda k, j, s, ad, fl: (0, 0, 0)))
    for b in range(blocks):
        in_specs.append(pl.BlockSpec((1, rank, BN), lambda k, j, s, ad, fl, b=b: (ad[b] // per_owner, 0, j)))
    return pl.pallas_call(
        functools.partial(final_kernel, per, len(lows)),
        grid_spec=pltpu.PrefetchScalarGridSpec(
            num_scalar_prefetch=3,
            grid=(2, steps),
            in_specs=in_specs,
            out_specs=pl.BlockSpec((rows, BN), lambda k, j, s, ad, fl: (k, j)),
        ),
        out_shape=jax.ShapeDtypeStruct(att.shape, jnp.bfloat16),
        compiler_params=params(),
        cost_estimate=COST,
    )(sched, adapters, fill, *[in_hbm(a) for a in (att, att_other, weight, weight_other, *pairs, *lows, *([expand_slots] * blocks))])


def after(a, *others):
    return lax.optimization_barrier((a, *others))[0]


def local(attended, out_weight, shrink_weight, expand_weight, block_adapter, block_fill):
    tokens, width = attended.shape
    owners = lax.axis_size("replica")
    n_tensor = lax.axis_size("tensor")
    chips = n_tensor // 2
    per_owner = shrink_weight.shape[0]
    half = tokens // 2
    t = lax.axis_index("tensor")
    x, c = t >> 1, t & 1

    i8 = jnp.arange(2 * chips, dtype=jnp.int32)
    sched = 2 * ((x + (i8 >> 1)) % chips) + ((c + i8) & 1)

    def send(a, chip_step):
        pairs = [(s, (s + 2 * chip_step) % n_tensor) for s in range(n_tensor)]
        return lax.ppermute(a, "tensor", pairs)

    def swap(a):
        return lax.ppermute(a, "tensor", [(s, s ^ 1) for s in range(n_tensor)])

    def exchange(a):
        return lax.all_to_all(a, "replica", 0, 0, tiled=True)

    OPP, NEXT, PREV, OWN = 4, 2, 6, 0

    owner_of = block_adapter // per_owner
    wanted = jnp.where(jnp.arange(owners)[:, None] == owner_of[None, :], (block_adapter - owner_of * per_owner)[None, :], 0)
    request = jnp.broadcast_to(jnp.sum(wanted, axis=1)[:, None, None], (owners, IDS, 128)).astype(jnp.int32)

    def lend(k):
        return swap(lax.dynamic_slice_in_dim(out_weight, sched[k + 1] * width, width, axis=1))

    att_other = swap(attended)
    opp_other = lend(OPP)
    served = exchange(request)[:, 0, 0]
    mm = functools.partial(matmuls, sched, attended, att_other, out_weight, half)

    opp_a, opp_b = mm([(OPP, 0, (opp_other, 0), ()), (OPP, half, (opp_other, 0), ())])
    right_1, left_1 = send(opp_a, 1), send(opp_b, -1)

    shrink_slots = exchange(shrink_weight[served])
    expand_slots = exchange(expand_weight[served])

    next_other, prev_other = lend(NEXT), lend(PREV)
    next_b, prev_a = mm([(NEXT, half, (next_other, 0), ()), (PREV, 0, (prev_other, 0), ())], deps=(opp_a,))
    next_b = after(next_b, right_1, left_1)
    right_2, left_2 = send(next_b, 1), send(prev_a, -1)
    next_a, prev_b = mm(
        [(NEXT, 0, (next_other, 0), ((right_1, 0),)), (PREV, half, (prev_other, 0), ((left_1, 0),))], deps=(next_b,)
    )
    own_other = lend(OWN)

    part = shrink(block_adapter, attended, shrink_slots, per_owner, deps=(next_a,))
    chip = (part.astype(jnp.float32) + swap(part).astype(jnp.float32)).astype(jnp.bfloat16)
    lows = [chip] + [send(chip, k) for k in range(1, chips)]

    next_a, prev_b, _, _ = lax.optimization_barrier((next_a, prev_b, right_2, left_2))
    right_3, left_3 = send(next_a, 1), send(prev_b, -1)

    pairs = (right_3, left_2, left_3, right_2)
    return finish(
        sched, block_adapter, block_fill, attended, att_other, out_weight, own_other, pairs, lows, expand_slots, per_owner
    )


def solution(mesh):
    in_specs = (
        P("replica", "tensor"),
        P("tensor", None),
        P("replica", None, "tensor"),
        P("replica", None, "tensor"),
        P("replica"),
        P("replica"),
    )
    out_specs = P("replica", "tensor")
    return jax.shard_map(local, mesh=mesh, in_specs=in_specs, out_specs=out_specs, check_vma=False)
```

time: 268 us -> 139 us (0.52)
  waiting for transfers between devices: 107 us -> 39.1 us
  blocking collectives: 68 us -> 14.4 us
  Pallas kernels: 0 us -> 45.6 us
  matrix products: 35.1 us -> 0 us
  between operations: 14.1 us -> 2.74 us
  other arithmetic: 10.8 us -> 0.17 us
  starting transfers between devices: 16.2 us -> 23 us
    unnamed x1 -> x0, blocking collectives: 68 us -> none
    all_to_all x2, waiting for transfers between devices: 60.9 us -> 8.44 us  [exchange(): return lax.all_to_all(a, 'replica', 0, 0, tiled=True)]
    pallas_call x0 -> x5, Pallas kernels: none -> 45.6 us  [the longest x3 30.4 us: matmuls(): pl.pallas_call(functools.partial(tasks_kernel, [len(t[3]) for t in tasks]...]
    dot_general x3 -> x0, matrix products: 35.1 us -> none  [the longest x1 25.8 us: local(): jnp.dot(attended, out_weight, preferred_element_type=jnp.float32)]
    ppermute x0 -> x15, waiting for transfers between devices: none -> 30.7 us  [the longest x9 29.3 us: send(): return lax.ppermute(a, 'tensor', pairs)]
    psum x1 -> x0, waiting for transfers between devices: 29.2 us -> none  [local(): low_rank = lax.psum(partial_low.astype(jnp.bfloat16), 'tensor')]
    reduce_scatter x1 -> x0, waiting for transfers between devices: 16.6 us -> none  [local(): lax.psum_scatter(partial_out.astype(jnp.bfloat16), 'tensor', scatter_dime...]
    all_to_all x0 -> x1, blocking collectives: none -> 14.4 us  [exchange(): return lax.all_to_all(a, 'replica', 0, 0, tiled=True)]
  transfers between devices with their start and end apart: 4 -> 17, of which waited for: 3 -> 7; matrix products, arithmetic and copies ran while one was open for 16% -> 9% of each run, Pallas kernels for 0% -> 24%
where the time goes in v1:
time: 139 us; the launch traced here: 138 us
  Pallas kernels  45.6 us (33%)
  waiting for transfers between devices  39.1 us (28%)
  starting transfers between devices  23 us (17%)
  blocking collectives  14.4 us (10%)
  local copies, waits for them, and re-layouts  13.2 us (9%)
  between operations  2.74 us (2%)
    pallas_call x3, Pallas kernels, matmuls(): pl.pallas_call(functools.partial(tasks_kernel, [len(t[3]) for t in tasks]...  30.4 us
    ppermute x9, waiting for transfers between devices, send(): return lax.ppermute(a, 'tensor', pairs)  29.3 us
    all_to_all x1, blocking collectives, exchange(): return lax.all_to_all(a, 'replica', 0, 0, tiled=True)  14.4 us
    all_to_all x2, starting transfers between devices, exchange(): return lax.all_to_all(a, 'replica', 0, 0, tiled=True)  12.9 us
    pallas_call x1, Pallas kernels, finish(): pl.pallas_call(functools.partial(final_kernel, per, len(lows)), grid_spec...  11.9 us
    ppermute x9, starting transfers between devices, send(): return lax.ppermute(a, 'tensor', pairs)  9.01 us
    all_to_all x2, waiting for transfers between devices, exchange(): return lax.all_to_all(a, 'replica', 0, 0, tiled=True)  8.44 us
    dynamic_slice x1, local copies, waits for them, and re-layouts, lend(): lax.dynamic_slice_in_dim(out_weight, sched[k + 1] * width, width, axis=1)  7.01 us
  transfers between devices with their start and end apart: 17, of which 7 were waited for; matrix products, arithmetic and copies ran while one was open for 9% of the time, Pallas kernels for 24%

profile of v1, /device:TPU:14, one launch (start us, length us, event | category | flops | bytes accessed | tf_op | source)
XLA Modules:
  0.0 138.2 jit_solution(8386260853848892138)
XLA Ops:
  0.0 0.7 fusion.4
  3.3 7.0 %constant_dynamic-slice_fusion = (bf16[1024,1024]{1,0:T(8,128)(2,1)}, bf16[1024,1024]{1,0:T(8,128)(2,1)}, bf16[1024,1024]{1,0:T(8,128)(2,1)}, bf16[1024,1024]{1,0:T(8,128)(2,1)}) fusion(bf16[1024,8192]{1,0:T(8,128)(2,1)} %w_ref.7, s32[]{:T(128)S(6)} %select_n.43, s32[]{:T(128)S(6)} %select_n.42, s32[]{:T(128)S(6)} %select_n.41, s32[]{:T(128)S(6)} %select_n.40), kind=kLoop, calls=%fused_computation.12 | loop fusion | bytes 16777232 | tf_op jit(solution)/shard_map/dynamic_slice | solution.py:219
  10.3 0.5 collective-permute-start.4
  10.8 0.5 collective-permute-start.3
  11.5 14.4 %all_to_all.15 = s32[16,1,128]{2,1,0:T(1,128)S(1)} all-to-all(s32[16,1,128]{2,1,0:T(1,128)S(1)} %broadcast_in_dim.16), channel_id=1, replica_groups=mesh['replica'=16,'tensor'=8] {'replica'}, dimensions={0} | all-to-all | bytes 16384 | tf_op jit(solution)/shard_map/all_to_all | solution.py:210
  25.9 0.4 slice_reduce_fusion
  26.3 2.1 %gather_fusion = bf16[16,64,1024]{2,1,0:T(8,128)(2,1)} fusion(bf16[12,64,1024]{2,1,0:T(8,128)(2,1)S(1)} %copy-done, s32[1024]{0:T(1024)S(1)} %pad_clamp_fusion), kind=kCustom, calls=%fused_computation | custom fusion | bytes 4194368 | tf_op jit(solution)/shard_map/gather | solution.py:229
  28.4 5.6 %all-to-all-start.1 = ((bf16[16,64,1024]{2,1,0:T(8,128)(2,1)}), bf16[16,64,1024]{2,1,0:T(8,128)(2,1)}, u32[]{:S(2)}, u32[]{:S(2)}) async-start(bf16[16,64,1024]{2,1,0:T(8,128)(2,1)} %gather_fusion), calls=%async_computation.1 | async-start | bytes 4194304 | tf_op jit(solution)/shard_map/all_to_all | solution.py:210
  34.0 10.1 %shard_map.64 = (bf16[512,1024]{1,0:T(8,128)(2,1)}, bf16[512,1024]{1,0:T(8,128)(2,1)}) custom-call(s32[8]{0:T(128)S(1)} %fusion.1.sched, bf16[1024,1024]{1,0:T(8,128)(2,1)} %a_ref.9, bf16[1024,1024]{1,0:T(8,128)(2,1)} %collective-permute-done.ap_ref, bf16[1024,8192]{1,0:T(8,128)(2,1)} %w_ref.7, bf16[1024,1024]{1,0:T(8,128)(2,1)} %collective-permute-done.4.refs_0_.refs_1_, ...), custom_call_target="tpu_custom_call" | custom-call | flops 10000000000 | bytes 10000000 | tf_op jit(solution)/shard_map/pallas_call | solution.py:78
  44.1 0.4 collective-permute-start.5
  44.5 1.7 %collective-permute-start.6 = (bf16[512,1024]{1,0:T(8,128)(2,1)}, bf16[512,1024]{1,0:T(8,128)(2,1)}, u32[]{:S(2)}, u32[]{:S(2)}) collective-permute-start(bf16[512,1024]{1,0:T(8,128)(2,1)} %get-tuple-element.15), channel_id=1, source_target_pairs={{0,6},{1,7},{2,0},{3,1},{4,2},{5,3},{6,4},{7,5},{8,14},{9,15},{10,... | collective-permute-start | bytes 3145736 | tf_op jit(solution)/shard_map/ppermute | solution.py:204
  46.1 10.0 %shard_map.65 = (bf16[512,1024]{1,0:T(8,128)(2,1)}, bf16[512,1024]{1,0:T(8,128)(2,1)}) custom-call(s32[8]{0:T(128)S(1)} %fusion.1.sched, bf16[1024,1024]{1,0:T(8,128)(2,1)} %a_ref.9, bf16[1024,1024]{1,0:T(8,128)(2,1)} %collective-permute-done.ap_ref, bf16[1024,8192]{1,0:T(8,128)(2,1)} %w_ref.7, bf16[1024,1024]{1,0:T(8,128)(2,1)} %collective-permute-done.2.refs_0_, ...), custom_call_target="tpu_custom_call" | custom-call | flops 10000000000 | bytes 10000000 | tf_op jit(solution)/shard_map/pallas_call | solution.py:78
  56.2 0.7 collective-permute-start.8
  56.9 10.9 %collective-permute-done.5.refs_2_ = bf16[512,1024]{1,0:T(8,128)(2,1)} collective-permute-done((bf16[512,1024]{1,0:T(8,128)(2,1)}, bf16[512,1024]{1,0:T(8,128)(2,1)}, u32[]{:S(2)}, u32[]{:S(2)}) %collective-permute-start.5) | collective-permute-done | bytes 1048608 | tf_op jit(solution)/shard_map/ppermute | solution.py:204
  67.8 4.3 %collective-permute-done.6.refs_3_ = bf16[512,1024]{1,0:T(8,128)(2,1)} collective-permute-done((bf16[512,1024]{1,0:T(8,128)(2,1)}, bf16[512,1024]{1,0:T(8,128)(2,1)}, u32[]{:S(2)}, u32[]{:S(2)}) %collective-permute-start.6) | collective-permute-done | bytes 1048608 | tf_op jit(solution)/shard_map/ppermute | solution.py:204
  72.1 0.4 collective-permute-start.7
  72.5 2.0 %gather_fusion.1 = bf16[16,64,1024]{2,1,0:T(8,128)(2,1)} fusion(bf16[12,64,1024]{2,1,0:T(8,128)(2,1)S(1)} %copy-done.3, s32[1024]{0:T(1024)S(1)} %pad_clamp_fusion), kind=kCustom, calls=%fused_computation.1 | custom fusion | bytes 4194368 | tf_op jit(solution)/shard_map/gather | solution.py:230
  74.5 7.3 %all-to-all-start.2 = ((bf16[16,64,1024]{2,1,0:T(8,128)(2,1)}), bf16[16,64,1024]{2,1,0:T(8,128)(2,1)}, u32[]{:S(2)}, u32[]{:S(2)}) async-start(bf16[16,64,1024]{2,1,0:T(8,128)(2,1)} %gather_fusion.1), calls=%async_computation.2 | async-start | bytes 4194304 | tf_op jit(solution)/shard_map/all_to_all | solution.py:210
  81.8 10.3 %shard_map.66 = (bf16[512,1024]{1,0:T(8,128)(2,1)}, bf16[512,1024]{1,0:T(8,128)(2,1)}) custom-call(s32[8]{0:T(128)S(1)} %fusion.1.sched, bf16[1024,1024]{1,0:T(8,128)(2,1)} %a_ref.9, bf16[1024,1024]{1,0:T(8,128)(2,1)} %collective-permute-done.ap_ref, bf16[1024,8192]{1,0:T(8,128)(2,1)} %w_ref.7, bf16[1024,1024]{1,0:T(8,128)(2,1)} %collective-permute-done.2.refs_0_, ...), custom_call_target="tpu_custom_call" | custom-call | flops 10000000000 | bytes 10000000 | tf_op jit(solution)/shard_map/pallas_call | solution.py:78
  92.1 1.5 %collective-permute-start.9 = (bf16[512,1024]{1,0:T(8,128)(2,1)}, bf16[512,1024]{1,0:T(8,128)(2,1)S(1)}, u32[]{:S(2)}, u32[]{:S(2)}) collective-permute-start(bf16[512,1024]{1,0:T(8,128)(2,1)} %get-tuple-element.21.refs_8_), channel_id=1, source_target_pairs={{0,2},{1,3},{2,4},{3,5},{4,6},{5,7},{6,0},{7,1},{8,10},{9,11},{10,... | collective-permute-start | bytes 3145736 | tf_op jit(solution)/shard_map/ppermute | solution.py:204
  93.5 0.6 collective-permute-start.10
  94.2 3.3 %shard_map.67 = bf16[8,64,128]{2,1,0:T(8,128)(2,1)S(1)} custom-call(s32[8]{0:T(128)S(1)} %copy-done.1, bf16[1024,1024]{1,0:T(8,128)(2,1)} %a_ref.9, bf16[16,64,1024]{2,1,0:T(8,128)(2,1)} %all-to-all-done.1.refs_0_.refs_1_.refs_2_.refs_3_.refs_4_.refs_5_.refs_6_.refs_7_, ...), custom_call_target="tpu_custom_call" | custom-call | flops 10000000000 | bytes 10000000 | tf_op jit(solution)/shard_map/pallas_call | solution.py:108
  97.6 1.3 collective-permute-done.11
  98.9 2.7 %collective-permute-start.12 = (bf16[8,64,128]{2,1,0:T(8,128)(2,1)S(1)}, bf16[8,64,128]{2,1,0:T(8,128)(2,1)S(1)}, u32[]{:S(2)}, u32[]{:S(2)}) collective-permute-start(bf16[8,64,128]{2,1,0:T(8,128)(2,1)S(1)} %add_convert_fusion.refs_4_), channel_id=1, source_target_pairs={{0,2},{1,3},{2,4},{3,5},{4,6},{5,7},{6,0},{7,1},{8,10},{9,11},{10,... | collective-permute-start | bytes 393224 | tf_op jit(solution)/shard_map/ppermute | solution.py:204
  101.6 1.1 collective-permute-start.13
  102.7 8.4 %all-to-all-done.2.refs_8_.refs_9_.refs_10_.refs_11_.refs_12_.refs_13_.refs_14_.refs_15_ = bf16[16,64,1024]{2,1,0:T(8,128)(2,1)} async-done(((bf16[16,64,1024]{2,1,0:T(8,128)(2,1)}), bf16[16,64,1024]{2,1,0:T(8,128)(2,1)}, u32[]{:S(2)}, u32[]{:S(2)}) %all-to-all-start.2) | async-done | bytes 2097184 | tf_op jit(solution)/shard_map/all_to_all | solution.py:210
  111.2 10.0 %collective-permute-done.12.refs_5_ = bf16[8,64,128]{2,1,0:T(8,128)(2,1)S(1)} collective-permute-done((bf16[8,64,128]{2,1,0:T(8,128)(2,1)S(1)}, bf16[8,64,128]{2,1,0:T(8,128)(2,1)S(1)}, u32[]{:S(2)}, u32[]{:S(2)}) %collective-permute-start.12) | collective-permute-done | bytes 131104 | tf_op jit(solution)/shard_map/ppermute | solution.py:204
  121.2 2.2 %collective-permute-done.13.refs_6_ = bf16[8,64,128]{2,1,0:T(8,128)(2,1)S(1)} collective-permute-done((bf16[8,64,128]{2,1,0:T(8,128)(2,1)S(1)}, bf16[8,64,128]{2,1,0:T(8,128)(2,1)S(1)}, u32[]{:S(2)}, u32[]{:S(2)}) %collective-permute-start.13) | collective-permute-done | bytes 131104 | tf_op jit(solution)/shard_map/ppermute | solution.py:204
  123.4 1.9 %collective-permute-done.14.refs_7_ = bf16[8,64,128]{2,1,0:T(8,128)(2,1)S(1)} collective-permute-done((bf16[8,64,128]{2,1,0:T(8,128)(2,1)S(1)}, bf16[8,64,128]{2,1,0:T(8,128)(2,1)S(1)}, u32[]{:S(2)}, u32[]{:S(2)}) %collective-permute-start.14) | collective-permute-done | bytes 131104 | tf_op jit(solution)/shard_map/ppermute | solution.py:204
  125.4 0.6 copy-done.8
  126.0 0.3 copy-done.4
  126.3 11.9 %shard_map.68 = bf16[1024,1024]{1,0:T(8,128)(2,1)} custom-call(s32[8]{0:T(128)S(1)} %fusion.1.sched, s32[8]{0:T(128)S(1)} %copy-done.1, s32[8]{0:T(128)S(1)} %copy-done.2, bf16[1024,1024]{1,0:T(8,128)(2,1)} %a_ref.9, bf16[1024,1024]{1,0:T(8,128)(2,1)} %collective-permute-done.ap_ref, bf16[1024,8192]{1,0:T(8,128)(2,1)} %w_ref.7, ...), custom_call_target="tpu_custom_call" | custom-call | flops 10000000000 | bytes 10000000 | tf_op jit(solution)/shard_map/pallas_call | solution.py:171
  (38 shorter events, 0.4 us)
Async XLA Ops:
  0.0 26.3 %copy-start = (bf16[12,64,1024]{2,1,0:T(8,128)(2,1)S(1)}, bf16[12,64,1024]{2,1,0:T(8,128)(2,1)}, u32[]{:S(2)}) copy-start(bf16[12,64,1024]{2,1,0:T(8,128)(2,1)} %param.8) | copy-start | bytes 4718596
  0.0 34.0 %collective-permute-start = (bf16[1024,1024]{1,0:T(8,128)(2,1)}, bf16[1024,1024]{1,0:T(8,128)(2,1)}, u32[]{:S(2)}, u32[]{:S(2)}) collective-permute-start(bf16[1024,1024]{1,0:T(8,128)(2,1)} %a_ref.9), channel_id=1, source_target_pairs={{0,1},{1,0},{2,3},{3,2},{4,5},{5,4},{6,7},{7,6},{8,9},{9,8},{10,11... | collective-permute-start | bytes 6291464 | tf_op jit(solution)/shard_map/ppermute | solution.py:207
  3.3 8.0 %copy-start.1 = (s32[8]{0:T(128)S(1)}, s32[8]{0:T(128)}, u32[]{:S(2)}) copy-start(s32[8]{0:T(128)} %adapters.3) | copy-start | bytes 100
  10.3 23.7 %collective-permute-start.4 = (bf16[1024,1024]{1,0:T(8,128)(2,1)}, bf16[1024,1024]{1,0:T(8,128)(2,1)}, u32[]{:S(2)}, u32[]{:S(2)}) collective-permute-start(bf16[1024,1024]{1,0:T(8,128)(2,1)} %get-tuple-element.25), channel_id=1, source_target_pairs={{0,1},{1,0},{2,3},{3,2},{4,5},{5,4},{6,7},{7,6},{8,9},{9,8},{10,11... | collective-permute-start | bytes 6291464 | tf_op jit(solution)/shard_map/ppermute | solution.py:207
  10.8 35.3 %collective-permute-start.2 = (bf16[1024,1024]{1,0:T(8,128)(2,1)}, bf16[1024,1024]{1,0:T(8,128)(2,1)}, u32[]{:S(2)}, u32[]{:S(2)}) collective-permute-start(bf16[1024,1024]{1,0:T(8,128)(2,1)} %get-tuple-element.27), channel_id=1, source_target_pairs={{0,1},{1,0},{2,3},{3,2},{4,5},{5,4},{6,7},{7,6},{8,9},{9,8},{10,11... | collective-permute-start | bytes 6291464 | tf_op jit(solution)/shard_map/ppermute | solution.py:207
  10.8 35.3 %collective-permute-start.3 = (bf16[1024,1024]{1,0:T(8,128)(2,1)}, bf16[1024,1024]{1,0:T(8,128)(2,1)}, u32[]{:S(2)}, u32[]{:S(2)}) collective-permute-start(bf16[1024,1024]{1,0:T(8,128)(2,1)} %get-tuple-element.26), channel_id=1, source_target_pairs={{0,1},{1,0},{2,3},{3,2},{4,5},{5,4},{6,7},{7,6},{8,9},{9,8},{10,11... | collective-permute-start | bytes 6291464 | tf_op jit(solution)/shard_map/ppermute | solution.py:207
  28.4 46.1 %all-to-all-start.1 = ((bf16[16,64,1024]{2,1,0:T(8,128)(2,1)}), bf16[16,64,1024]{2,1,0:T(8,128)(2,1)}, u32[]{:S(2)}, u32[]{:S(2)}) async-start(bf16[16,64,1024]{2,1,0:T(8,128)(2,1)} %gather_fusion), calls=%async_computation.1 | async-start | bytes 4194304 | tf_op jit(solution)/shard_map/all_to_all | solution.py:210
  44.1 23.7 %collective-permute-start.5 = (bf16[512,1024]{1,0:T(8,128)(2,1)}, bf16[512,1024]{1,0:T(8,128)(2,1)}, u32[]{:S(2)}, u32[]{:S(2)}) collective-permute-start(bf16[512,1024]{1,0:T(8,128)(2,1)} %get-tuple-element.14.refs_2_), channel_id=1, source_target_pairs={{0,2},{1,3},{2,4},{3,5},{4,6},{5,7},{6,0},{7,1},{8,10},{9,11},{10,... | collective-permute-start | bytes 3145736 | tf_op jit(solution)/shard_map/ppermute | solution.py:204
  44.5 28.0 %copy-start.3 = (bf16[12,64,1024]{2,1,0:T(8,128)(2,1)S(1)}, bf16[12,64,1024]{2,1,0:T(8,128)(2,1)}, u32[]{:S(2)}) copy-start(bf16[12,64,1024]{2,1,0:T(8,128)(2,1)} %param.9) | copy-start | bytes 4718596
  44.5 27.6 %collective-permute-start.6 = (bf16[512,1024]{1,0:T(8,128)(2,1)}, bf16[512,1024]{1,0:T(8,128)(2,1)}, u32[]{:S(2)}, u32[]{:S(2)}) collective-permute-start(bf16[512,1024]{1,0:T(8,128)(2,1)} %get-tuple-element.15), channel_id=1, source_target_pairs={{0,6},{1,7},{2,0},{3,1},{4,2},{5,3},{6,4},{7,5},{8,14},{9,15},{10,... | collective-permute-start | bytes 3145736 | tf_op jit(solution)/shard_map/ppermute | solution.py:204
  56.2 35.9 %collective-permute-start.8 = (bf16[512,1024]{1,0:T(8,128)(2,1)}, bf16[512,1024]{1,0:T(8,128)(2,1)}, u32[]{:S(2)}, u32[]{:S(2)}) collective-permute-start(bf16[512,1024]{1,0:T(8,128)(2,1)} %get-tuple-element.20), channel_id=1, source_target_pairs={{0,6},{1,7},{2,0},{3,1},{4,2},{5,3},{6,4},{7,5},{8,14},{9,15},{10,... | collective-permute-start | bytes 3145736 | tf_op jit(solution)/shard_map/ppermute | solution.py:204
  72.1 20.0 %collective-permute-start.7 = (bf16[512,1024]{1,0:T(8,128)(2,1)}, bf16[512,1024]{1,0:T(8,128)(2,1)}, u32[]{:S(2)}, u32[]{:S(2)}) collective-permute-start(bf16[512,1024]{1,0:T(8,128)(2,1)} %get-tuple-element.17.refs_4_), channel_id=1, source_target_pairs={{0,2},{1,3},{2,4},{3,5},{4,6},{5,7},{6,0},{7,1},{8,10},{9,11},{10,... | collective-permute-start | bytes 3145736 | tf_op jit(solution)/shard_map/ppermute | solution.py:204
  72.5 30.3 %collective-permute-start.1 = (bf16[1024,1024]{1,0:T(8,128)(2,1)}, bf16[1024,1024]{1,0:T(8,128)(2,1)}, u32[]{:S(2)}, u32[]{:S(2)}) collective-permute-start(bf16[1024,1024]{1,0:T(8,128)(2,1)} %get-tuple-element.28), channel_id=1, source_target_pairs={{0,1},{1,0},{2,3},{3,2},{4,5},{5,4},{6,7},{7,6},{8,9},{9,8},{10,11... | collective-permute-start | bytes 6291464 | tf_op jit(solution)/shard_map/ppermute | solution.py:207
  74.5 36.7 %all-to-all-start.2 = ((bf16[16,64,1024]{2,1,0:T(8,128)(2,1)}), bf16[16,64,1024]{2,1,0:T(8,128)(2,1)}, u32[]{:S(2)}, u32[]{:S(2)}) async-start(bf16[16,64,1024]{2,1,0:T(8,128)(2,1)} %gather_fusion.1), calls=%async_computation.2 | async-start | bytes 4194304 | tf_op jit(solution)/shard_map/all_to_all | solution.py:210
  92.1 34.3 %copy-start.2 = (s32[8]{0:T(128)S(1)}, s32[8]{0:T(128)}, u32[]{:S(2)}) copy-start(s32[8]{0:T(128)} %fill.1) | copy-start | bytes 100
  92.1 33.2 %collective-permute-start.9 = (bf16[512,1024]{1,0:T(8,128)(2,1)}, bf16[512,1024]{1,0:T(8,128)(2,1)S(1)}, u32[]{:S(2)}, u32[]{:S(2)}) collective-permute-start(bf16[512,1024]{1,0:T(8,128)(2,1)} %get-tuple-element.21.refs_8_), channel_id=1, source_target_pairs={{0,2},{1,3},{2,4},{3,5},{4,6},{5,7},{6,0},{7,1},{8,10},{9,11},{10,... | collective-permute-start | bytes 3145736 | tf_op jit(solution)/shard_map/ppermute | solution.py:204
  93.5 31.8 %collective-permute-start.10 = (bf16[512,1024]{1,0:T(8,128)(2,1)}, bf16[512,1024]{1,0:T(8,128)(2,1)}, u32[]{:S(2)}, u32[]{:S(2)}) collective-permute-start(bf16[512,1024]{1,0:T(8,128)(2,1)} %get-tuple-element.22), channel_id=1, source_target_pairs={{0,6},{1,7},{2,0},{3,1},{4,2},{5,3},{6,4},{7,5},{8,14},{9,15},{10,... | collective-permute-start | bytes 3145736 | tf_op jit(solution)/shard_map/ppermute | solution.py:204
  97.5 1.4 %collective-permute-start.11 = (bf16[8,64,128]{2,1,0:T(8,128)(2,1)S(1)}, bf16[8,64,128]{2,1,0:T(8,128)(2,1)S(1)}, u32[]{:S(2)}, u32[]{:S(2)}) collective-permute-start(bf16[8,64,128]{2,1,0:T(8,128)(2,1)S(1)} %shard_map.67), channel_id=1, source_target_pairs={{0,1},{1,0},{2,3},{3,2},{4,5},{5,4},{6,7},{7,6},{8,9},{9,8},{10,11... | collective-permute-start | bytes 393224 | tf_op jit(solution)/shard_map/ppermute | solution.py:207
  98.9 26.4 %copy-start.5 = (bf16[8,64,128]{2,1,0:T(8,128)(2,1)}, bf16[8,64,128]{2,1,0:T(8,128)(2,1)S(1)}, u32[]{:S(2)}) copy-start(bf16[8,64,128]{2,1,0:T(8,128)(2,1)S(1)} %add_convert_fusion.refs_4_) | copy-start | bytes 393220
  98.9 22.3 %collective-permute-start.12 = (bf16[8,64,128]{2,1,0:T(8,128)(2,1)S(1)}, bf16[8,64,128]{2,1,0:T(8,128)(2,1)S(1)}, u32[]{:S(2)}, u32[]{:S(2)}) collective-permute-start(bf16[8,64,128]{2,1,0:T(8,128)(2,1)S(1)} %add_convert_fusion.refs_4_), channel_id=1, source_target_pairs={{0,2},{1,3},{2,4},{3,5},{4,6},{5,7},{6,0},{7,1},{8,10},{9,11},{10,... | collective-permute-start | bytes 393224 | tf_op jit(solution)/shard_map/ppermute | solution.py:204
  101.6 21.8 %collective-permute-start.13 = (bf16[8,64,128]{2,1,0:T(8,128)(2,1)S(1)}, bf16[8,64,128]{2,1,0:T(8,128)(2,1)S(1)}, u32[]{:S(2)}, u32[]{:S(2)}) collective-permute-start(bf16[8,64,128]{2,1,0:T(8,128)(2,1)S(1)} %add_convert_fusion.refs_4_), channel_id=1, source_target_pairs={{0,4},{1,5},{2,6},{3,7},{4,0},{5,1},{6,2},{7,3},{8,12},{9,13},{10,... | collective-permute-start | bytes 393224 | tf_op jit(solution)/shard_map/ppermute | solution.py:204
  102.7 22.6 %collective-permute-start.14 = (bf16[8,64,128]{2,1,0:T(8,128)(2,1)S(1)}, bf16[8,64,128]{2,1,0:T(8,128)(2,1)S(1)}, u32[]{:S(2)}, u32[]{:S(2)}) collective-permute-start(bf16[8,64,128]{2,1,0:T(8,128)(2,1)S(1)} %add_convert_fusion.refs_4_), channel_id=1, source_target_pairs={{0,6},{1,7},{2,0},{3,1},{4,2},{5,3},{6,4},{7,5},{8,14},{9,15},{10,... | collective-permute-start | bytes 393224 | tf_op jit(solution)/shard_map/ppermute | solution.py:204
  121.2 4.1 %copy-start.6 = (bf16[8,64,128]{2,1,0:T(8,128)(2,1)}, bf16[8,64,128]{2,1,0:T(8,128)(2,1)S(1)}, u32[]{:S(2)}) copy-start(bf16[8,64,128]{2,1,0:T(8,128)(2,1)S(1)} %collective-permute-done.12.refs_5_) | copy-start | bytes 393220
  123.4 2.0 %copy-start.7 = (bf16[8,64,128]{2,1,0:T(8,128)(2,1)}, bf16[8,64,128]{2,1,0:T(8,128)(2,1)S(1)}, u32[]{:S(2)}) copy-start(bf16[8,64,128]{2,1,0:T(8,128)(2,1)S(1)} %collective-permute-done.13.refs_6_) | copy-start | bytes 393220
  125.3 0.7 copy-start.8
  125.3 1.0 copy-start.4

commit v2 on v1

v2 whole, which is shorter than its diff:
```python
import functools

import jax
import jax.numpy as jnp
from jax import lax
from jax.experimental import pallas as pl
from jax.experimental.pallas import tpu as pltpu
from jax.sharding import PartitionSpec as P

BN = 512
IDS = 1
COST = pl.CostEstimate(flops=10000000000,bytes_accessed=10000000, transcendentals=0)


def any_spec():
    return pl.BlockSpec(memory_space=pl.ANY)


def in_hbm(a):
    return pltpu.with_memory_space_constraint(a, pltpu.HBM)


def params():
    return pltpu.CompilerParams(vmem_limit_bytes=20 * 1024 * 1024)


def choose(values, k):
    out = values[-1]
    for i in range(len(values) - 2, -1, -1):
        out = jnp.where(k == i, values[i], out) if values[i] is not out else out
    return out


def clamp(g, steps, k):
    return jnp.clip(g - k * steps, 0, steps - 1)


def tasks_kernel(tasks, steps, sched, a_ref, ap_ref, w_ref, wp_ref, *refs):
    n = len(tasks)
    outs = refs[-n:]
    at = 0
    for k, count in enumerate(tasks):
        mine = refs[at:at + count]
        at += count

        @pl.when(pl.program_id(0) // steps == k)
        def _(k=k, mine=mine):
            acc = jnp.dot(a_ref[...], w_ref[...], preferred_element_type=jnp.float32)
            acc = acc + jnp.dot(ap_ref[...], wp_ref[...], preferred_element_type=jnp.float32)
            for add in mine:
                acc = acc + add[...].astype(jnp.float32)
            outs[k][...] = acc.astype(outs[k].dtype)


def matmuls(sched, att, att_other, weight, weight_other, rows, tasks, deps=()):
    width = att.shape[1]
    depth = weight.shape[0]
    steps = width // BN
    alone = weight_other.shape[1] == width

    def a_map(g, s):
        return (choose([t[1] // rows for t in tasks], g // steps), 0)

    def w_map(g, s):
        slot = choose([t[0] for t in tasks], g // steps)
        return (0, s[slot] * steps + g % steps)

    in_specs = [
        pl.BlockSpec((rows, width), a_map),
        pl.BlockSpec((rows, width), a_map),
        pl.BlockSpec((depth, BN), w_map),
        pl.BlockSpec((depth, BN), (lambda g, s: (0, g % steps)) if alone else w_map),
    ]
    operands = [att, att_other, weight, weight_other]
    for k, task in enumerate(tasks):
        for array, row in task[2]:
            in_specs.append(pl.BlockSpec((rows, BN), lambda g, s, k=k, row=row: (row // rows, clamp(g, steps, k))))
            operands.append(array)
    in_specs += [any_spec() for _ in deps]
    return pl.pallas_call(
        functools.partial(tasks_kernel, [len(t[2]) for t in tasks], steps),
        grid_spec=pltpu.PrefetchScalarGridSpec(
            num_scalar_prefetch=1,
            grid=(steps * len(tasks),),
            in_specs=in_specs,
            out_specs=[pl.BlockSpec((rows, BN), lambda g, s, k=k: (0, clamp(g, steps, k))) for k in range(len(tasks))],
        ),
        out_shape=[pltpu.HBM((rows, width), jnp.bfloat16) for _ in tasks],
        compiler_params=params(),
        cost_estimate=COST,
    )(sched, *[in_hbm(a) for a in operands], *[in_hbm(a) for a in deps])


def shrink_kernel(blocks, rows, adapters, a_ref, *refs):
    o_ref = refs[-1]
    for b in range(blocks):
        o_ref[b] = lax.dot_general(
            refs[b][0], a_ref[b * rows:(b + 1) * rows, :], (((1,), (1,)), ((), ())), preferred_element_type=jnp.float32
        ).astype(o_ref.dtype)


def shrink(adapters, att, slots, per_owner, deps=()):
    blocks = adapters.shape[0]
    rows = att.shape[0] // blocks
    _, rank, width = slots.shape
    in_specs = [pl.BlockSpec(att.shape, lambda g, ad: (0, 0))]
    for b in range(blocks):
        in_specs.append(pl.BlockSpec((1, rank, width), lambda g, ad, b=b: (ad[b] // per_owner, 0, 0)))
    in_specs += [any_spec() for _ in deps]
    return pl.pallas_call(
        functools.partial(shrink_kernel, blocks, rows),
        grid_spec=pltpu.PrefetchScalarGridSpec(
            num_scalar_prefetch=1,
            grid=(1,),
            in_specs=in_specs,
            out_specs=pl.BlockSpec((blocks, rank, rows), lambda g, ad: (0, 0, 0)),
        ),
        out_shape=jax.ShapeDtypeStruct((blocks, rank, rows), jnp.bfloat16),
        compiler_params=params(),
        cost_estimate=COST,
    )(adapters, in_hbm(att), *([in_hbm(slots)] * blocks), *[in_hbm(a) for a in deps])


def final_kernel(per, n_low, adapters, fill, *refs):
    parts, refs = refs[:4], refs[4:]
    lows, refs = refs[:n_low], refs[n_low:]
    expands, o_ref = refs[:2 * per], refs[-1]
    block = parts[0].shape[0] // per
    for k in range(2):

        @pl.when(pl.program_id(0) == k)
        def _(k=k):
            for i in range(per):
                b = k * per + i
                rows = slice(i * block, (i + 1) * block)
                low = lows[0][b].astype(jnp.float32)
                for other in lows[1:]:
                    low = low + other[b].astype(jnp.float32)
                delta = lax.dot_general(
                    low.astype(jnp.bfloat16), expands[b][0], (((0,), (0,)), ((), ())), preferred_element_type=jnp.float32
                ).astype(jnp.bfloat16)
                base = parts[2 * k][rows, :].astype(jnp.float32) + parts[2 * k + 1][rows, :].astype(jnp.float32)
                out = base + delta.astype(jnp.float32)
                live = lax.broadcasted_iota(jnp.int32, out.shape, 0) < fill[b]
                o_ref[rows, :] = jnp.where(live, out, 0.0).astype(o_ref.dtype)


def finish(adapters, fill, parts, lows, expand_slots, per_owner):
    blocks = adapters.shape[0]
    rows, width = parts[0].shape
    steps = width // BN
    per = blocks // 2
    rank = expand_slots.shape[1]
    in_specs = []
    for k0 in range(2):
        for _ in range(2):
            in_specs.append(pl.BlockSpec((rows, BN), lambda k, j, ad, fl, k0=k0: (0, clamp(k * steps + j, steps, k0))))
    for low in lows:
        in_specs.append(pl.BlockSpec(low.shape, lambda k, j, ad, fl: (0, 0, 0)))
    for b in range(blocks):
        in_specs.append(
            pl.BlockSpec(
                (1, rank, BN),
                lambda k, j, ad, fl, b=b: (ad[b] // per_owner, 0, clamp(k * steps + j, steps, b // per)),
            )
        )
    return pl.pallas_call(
        functools.partial(final_kernel, per, len(lows)),
        grid_spec=pltpu.PrefetchScalarGridSpec(
            num_scalar_prefetch=2,
            grid=(2, steps),
            in_specs=in_specs,
            out_specs=pl.BlockSpec((rows, BN), lambda k, j, ad, fl: (k, j)),
        ),
        out_shape=jax.ShapeDtypeStruct((2 * rows, width), jnp.bfloat16),
        compiler_params=params(),
        cost_estimate=COST,
    )(adapters, fill, *[in_hbm(a) for a in (*parts, *lows, *([expand_slots] * blocks))])


def after(a, *others):
    return lax.optimization_barrier((a, *others))[0]


def local(attended, out_weight, shrink_weight, expand_weight, block_adapter, block_fill):
    tokens, width = attended.shape
    owners = lax.axis_size("replica")
    n_tensor = lax.axis_size("tensor")
    chips = n_tensor // 2
    per_owner = shrink_weight.shape[0]
    half = tokens // 2
    t = lax.axis_index("tensor")
    x, c = t >> 1, t & 1

    i8 = jnp.arange(2 * chips, dtype=jnp.int32)
    sched = 2 * ((x + (i8 >> 1)) % chips) + ((c + i8) & 1)

    def send(a, chip_step):
        pairs = [(s, (s + 2 * chip_step) % n_tensor) for s in range(n_tensor)]
        return lax.ppermute(a, "tensor", pairs)

    def swap(a):
        return lax.ppermute(a, "tensor", [(s, s ^ 1) for s in range(n_tensor)])

    def exchange(a):
        return lax.all_to_all(a, "replica", 0, 0, tiled=True)

    OPP, NEXT, PREV, OWN = 4, 2, 6, 0

    owner_of = block_adapter // per_owner
    wanted = jnp.where(jnp.arange(owners)[:, None] == owner_of[None, :], (block_adapter - owner_of * per_owner)[None, :], 0)
    request = jnp.broadcast_to(jnp.sum(wanted, axis=1)[:, None, None], (owners, IDS, 128)).astype(jnp.int32)

    att_other = swap(attended)
    start = (2 * lax.rem(x + OPP // 2, chips) + (1 - c)) * width
    opp_piece = lax.dynamic_slice_in_dim(out_weight, start, width, axis=1)
    opp_other = swap(opp_piece)
    asked = exchange(after(request, opp_piece))
    weight_other = swap(after(out_weight, opp_other, att_other))
    mm = functools.partial(matmuls, sched, attended, att_other, out_weight)

    opp_a, opp_b = mm(opp_other, half, [(OPP, 0, ()), (OPP, half, ())], deps=(asked,))
    right_1, left_1 = send(opp_a, 1), send(opp_b, -1)

    served = after(asked[:, 0, 0], opp_a)
    shrink_slots = exchange(shrink_weight[served])
    expand_slots = exchange(expand_weight[served])

    mm = functools.partial(mm, weight_other, half)
    next_b, prev_a = mm([(NEXT, half, ()), (PREV, 0, ())], deps=(opp_a,))
    right_2, left_2 = send(next_b, 1), send(prev_a, -1)
    next_a, prev_b = mm([(NEXT, 0, ((right_1, 0),)), (PREV, half, ((left_1, 0),))], deps=(next_b,))

    part = shrink(block_adapter, attended, shrink_slots, per_owner, deps=(next_a,))
    chip = (part.astype(jnp.float32) + swap(part).astype(jnp.float32)).astype(jnp.bfloat16)
    lows = [chip] + [send(chip, k) for k in range(1, chips)]

    next_a, prev_b, _, _ = lax.optimization_barrier((next_a, prev_b, right_2, left_2))
    right_3, left_3 = send(next_a, 1), send(prev_b, -1)

    own_a, own_b = mm([(OWN, 0, ((left_2, 0),)), (OWN, half, ((right_2, 0),))], deps=(next_a,))
    return finish(block_adapter, block_fill, (own_a, right_3, own_b, left_3), lows, expand_slots, per_owner)


def solution(mesh):
    in_specs = (
        P("replica", "tensor"),
        P("tensor", None),
        P("replica", None, "tensor"),
        P("replica", None, "tensor"),
        P("replica"),
        P("replica"),
    )
    out_specs = P("replica", "tensor")
    return jax.shard_map(local, mesh=mesh, in_specs=in_specs, out_specs=out_specs, check_vma=False)
```

time: 139 us -> 123 us (0.88)
  blocking collectives: 14.4 us -> 0 us
  starting transfers between devices: 23 us -> 32.3 us
  waiting for transfers between devices: 39.1 us -> 30.7 us
  Pallas kernels: 45.6 us -> 50.2 us
  local copies, waits for them, and re-layouts: 13.2 us -> 9.12 us
  between operations: 2.74 us -> 0.3 us
    ppermute x9, waiting for transfers between devices: 29.3 us -> 14.1 us  [send(): return lax.ppermute(a, 'tensor', pairs)]
    all_to_all x1 -> x0, blocking collectives: 14.4 us -> none  [exchange(): return lax.all_to_all(a, 'replica', 0, 0, tiled=True)]
    pallas_call x3 -> x4, Pallas kernels: 30.4 us -> 40.7 us  [matmuls(): pl.pallas_call(functools.partial(tasks_kernel, [len(t[2]) for t in tasks]...]
    all_to_all x2 -> x3, starting transfers between devices: 12.9 us -> 20.6 us  [exchange(): return lax.all_to_all(a, 'replica', 0, 0, tiled=True)]
    pallas_call x1, Pallas kernels: 11.9 us -> 6.22 us  [finish(): pl.pallas_call(functools.partial(final_kernel, per, len(lows)), grid_spec...]
    dynamic_slice x1, local copies, waits for them, and re-layouts: 7.01 us -> 1.88 us  [local(): opp_piece = lax.dynamic_slice_in_dim(out_weight, start, width, axis=1)]
    ppermute x6 -> x4, waiting for transfers between devices: 1.35 us -> 4.79 us  [swap(): return lax.ppermute(a, 'tensor', [(s, s ^ 1) for s in range(n_tensor)])]
    all_to_all x2 -> x3, waiting for transfers between devices: 8.44 us -> 11.8 us  [exchange(): return lax.all_to_all(a, 'replica', 0, 0, tiled=True)]
  transfers between devices with their start and end apart: 17 -> 16, of which waited for: 7 -> 9; matrix products, arithmetic and copies ran while one was open for 9% -> 6% of each run, Pallas kernels for 24% -> 36%
where the time goes in v2:
time: 123 us
  Pallas kernels  50.2 us (41%)
  starting transfers between devices  32.3 us (26%)
  waiting for transfers between devices  30.7 us (25%)
  local copies, waits for them, and re-layouts  9.12 us (7%)
    pallas_call x4, Pallas kernels, matmuls(): pl.pallas_call(functools.partial(tasks_kernel, [len(t[2]) for t in tasks]...  40.7 us
    all_to_all x3, starting transfers between devices, exchange(): return lax.all_to_all(a, 'replica', 0, 0, tiled=True)  20.6 us
    ppermute x9, waiting for transfers between devices, send(): return lax.ppermute(a, 'tensor', pairs)  14.1 us
    all_to_all x3, waiting for transfers between devices, exchange(): return lax.all_to_all(a, 'replica', 0, 0, tiled=True)  11.8 us
    ppermute x9, starting transfers between devices, send(): return lax.ppermute(a, 'tensor', pairs)  11 us
    pallas_call x1, Pallas kernels, finish(): pl.pallas_call(functools.partial(final_kernel, per, len(lows)), grid_spec...  6.22 us
    ppermute x4, waiting for transfers between devices, swap(): return lax.ppermute(a, 'tensor', [(s, s ^ 1) for s in range(n_tensor)])  4.79 us
    pallas_call x1, Pallas kernels, shrink(): pl.pallas_call(functools.partial(shrink_kernel, blocks, rows), grid_spec=...  3.29 us
  transfers between devices with their start and end apart: 16, of which 9 were waited for; matrix products, arithmetic and copies ran while one was open for 6% of the time, Pallas kernels for 36%

profile of v2, /device:TPU:14, one launch (start us, length us, event | category | flops | bytes accessed | tf_op | source)
XLA Modules:
  0.0 122.9 jit_solution(199636058013101426)
XLA Ops:
  0.0 1.9 %constant_dynamic-slice_fusion = bf16[1024,1024]{1,0:T(8,128)(2,1)S(1)} fusion(bf16[1024,8192]{1,0:T(8,128)(2,1)} %w_ref.7, s32[]{:T(128)S(6)} %select_n.24), kind=kLoop, calls=%fused_computation.16 | loop fusion | bytes 4194308 | tf_op jit(solution)/shard_map/dynamic_slice | solution.py:216
  2.4 2.1 %collective-permute-done.ap_ref = bf16[1024,1024]{1,0:T(8,128)(2,1)} collective-permute-done((bf16[1024,1024]{1,0:T(8,128)(2,1)}, bf16[1024,1024]{1,0:T(8,128)(2,1)}, u32[]{:S(2)}, u32[]{:S(2)}) %collective-permute-start) | collective-permute-done | bytes 2097184 | tf_op jit(solution)/shard_map/ppermute | solution.py:203
  4.5 2.7 %collective-permute-done.1.wp_ref = bf16[1024,1024]{1,0:T(8,128)(2,1)S(1)} collective-permute-done((bf16[1024,1024]{1,0:T(8,128)(2,1)S(1)}, bf16[1024,1024]{1,0:T(8,128)(2,1)S(1)}, u32[]{:S(2)}, u32[]{:S(2)}) %collective-permute-start.1) | collective-permute-done | bytes 2097184 | tf_op jit(solution)/shard_map/ppermute | solution.py:203
  7.2 1.3 %copy-done.9 = bf16[1024,1024]{1,0:T(8,128)(2,1)} copy-done((bf16[1024,1024]{1,0:T(8,128)(2,1)}, bf16[1024,1024]{1,0:T(8,128)(2,1)S(1)}, u32[]{:S(2)}) %copy-start.9) | copy-done | bytes 2097176
  8.7 0.7 broadcast_in_dim.27
  9.4 8.4 %all-to-all-start = ((s32[16,1,128]{2,1,0:T(1,128)}), s32[16,1,128]{2,1,0:T(1,128)S(1)}, u32[]{:S(2)}, u32[]{:S(2)}) async-start(s32[16,1,128]{2,1,0:T(1,128)} %broadcast_in_dim.27), calls=%async_computation | async-start | bytes 16384 | tf_op jit(solution)/shard_map/all_to_all | solution.py:206
  17.8 6.2 %all-to-all-done.refs_0_ = s32[16,1,128]{2,1,0:T(1,128)S(1)} async-done(((s32[16,1,128]{2,1,0:T(1,128)}), s32[16,1,128]{2,1,0:T(1,128)S(1)}, u32[]{:S(2)}, u32[]{:S(2)}) %all-to-all-start) | async-done | bytes 8224 | tf_op jit(solution)/shard_map/all_to_all | solution.py:206
  24.6 10.0 %shard_map.64 = (bf16[512,1024]{1,0:T(8,128)(2,1)}, bf16[512,1024]{1,0:T(8,128)(2,1)}) custom-call(s32[8]{0:T(128)S(1)} %fusion.1.sched, bf16[1024,1024]{1,0:T(8,128)(2,1)} %a_ref.9, bf16[1024,1024]{1,0:T(8,128)(2,1)} %collective-permute-done.ap_ref, bf16[1024,8192]{1,0:T(8,128)(2,1)} %w_ref.7, bf16[1024,1024]{1,0:T(8,128)(2,1)} %copy-done.9, ...), custom_call_target="tpu_custom_call" | custom-call | flops 10000000000 | bytes 10000000 | tf_op jit(solution)/shard_map/pallas_call | solution.py:80
  34.6 0.5 collective-permute-start.5
  35.1 1.5 %collective-permute-start.6 = (bf16[512,1024]{1,0:T(8,128)(2,1)}, bf16[512,1024]{1,0:T(8,128)(2,1)}, u32[]{:S(2)}, u32[]{:S(2)}) collective-permute-start(bf16[512,1024]{1,0:T(8,128)(2,1)} %get-tuple-element.23), channel_id=1, source_target_pairs={{0,6},{1,7},{2,0},{3,1},{4,2},{5,3},{6,4},{7,5},{8,14},{9,15},{10,... | collective-permute-start | bytes 3145736 | tf_op jit(solution)/shard_map/ppermute | solution.py:200
  36.7 2.0 %gather_fusion = bf16[16,64,1024]{2,1,0:T(8,128)(2,1)} fusion(bf16[12,64,1024]{2,1,0:T(8,128)(2,1)S(1)} %copy-done, s32[1024]{0:T(1024)S(1)} %pad_clamp_fusion), kind=kCustom, calls=%fused_computation | custom fusion | bytes 4194368 | tf_op jit(solution)/shard_map/gather | solution.py:226
  38.7 5.6 %all-to-all-start.1 = ((bf16[16,64,1024]{2,1,0:T(8,128)(2,1)}), bf16[16,64,1024]{2,1,0:T(8,128)(2,1)}, u32[]{:S(2)}, u32[]{:S(2)}) async-start(bf16[16,64,1024]{2,1,0:T(8,128)(2,1)} %gather_fusion), calls=%async_computation.1 | async-start | bytes 4194304 | tf_op jit(solution)/shard_map/all_to_all | solution.py:206
  44.3 2.0 %gather_fusion.1 = bf16[16,64,1024]{2,1,0:T(8,128)(2,1)} fusion(bf16[12,64,1024]{2,1,0:T(8,128)(2,1)S(1)} %copy-done.4, s32[1024]{0:T(1024)S(1)} %pad_clamp_fusion), kind=kCustom, calls=%fused_computation.1 | custom fusion | bytes 4194368 | tf_op jit(solution)/shard_map/gather | solution.py:227
  46.3 10.0 %shard_map.65 = (bf16[512,1024]{1,0:T(8,128)(2,1)}, bf16[512,1024]{1,0:T(8,128)(2,1)}) custom-call(s32[8]{0:T(128)S(1)} %fusion.1.sched, bf16[1024,1024]{1,0:T(8,128)(2,1)} %a_ref.9, bf16[1024,1024]{1,0:T(8,128)(2,1)} %collective-permute-done.ap_ref, bf16[1024,8192]{1,0:T(8,128)(2,1)} %w_ref.7, bf16[1024,8192]{1,0:T(8,128)(2,1)} %collective-permute-done.2.wp_ref, ...), custom_call_target="tpu_custom_call" | custom-call | flops 10000000000 | bytes 10000000 | tf_op jit(solution)/shard_map/pallas_call | solution.py:80
  56.3 0.8 collective-permute-start.3
  57.1 2.4 %collective-permute-start.4 = (bf16[512,1024]{1,0:T(8,128)(2,1)}, bf16[512,1024]{1,0:T(8,128)(2,1)}, u32[]{:S(2)}, u32[]{:S(2)}) collective-permute-start(bf16[512,1024]{1,0:T(8,128)(2,1)} %get-tuple-element.22.refs_2_), channel_id=1, source_target_pairs={{0,2},{1,3},{2,4},{3,5},{4,6},{5,7},{6,0},{7,1},{8,10},{9,11},{10,... | collective-permute-start | bytes 3145736 | tf_op jit(solution)/shard_map/ppermute | solution.py:200
  59.6 2.1 %collective-permute-done.6.refs_1_ = bf16[512,1024]{1,0:T(8,128)(2,1)} collective-permute-done((bf16[512,1024]{1,0:T(8,128)(2,1)}, bf16[512,1024]{1,0:T(8,128)(2,1)}, u32[]{:S(2)}, u32[]{:S(2)}) %collective-permute-start.6) | collective-permute-done | bytes 1048608 | tf_op jit(solution)/shard_map/ppermute | solution.py:200
  61.7 10.3 %shard_map.66 = (bf16[512,1024]{1,0:T(8,128)(2,1)}, bf16[512,1024]{1,0:T(8,128)(2,1)}) custom-call(s32[8]{0:T(128)S(1)} %fusion.1.sched, bf16[1024,1024]{1,0:T(8,128)(2,1)} %a_ref.9, bf16[1024,1024]{1,0:T(8,128)(2,1)} %collective-permute-done.ap_ref, bf16[1024,8192]{1,0:T(8,128)(2,1)} %w_ref.7, bf16[1024,8192]{1,0:T(8,128)(2,1)} %collective-permute-done.2.wp_ref, ...), custom_call_target="tpu_custom_call" | custom-call | flops 10000000000 | bytes 10000000 | tf_op jit(solution)/shard_map/pallas_call | solution.py:80
  72.0 6.6 %all-to-all-start.2 = ((bf16[16,64,1024]{2,1,0:T(8,128)(2,1)}), bf16[16,64,1024]{2,1,0:T(8,128)(2,1)}, u32[]{:S(2)}, u32[]{:S(2)}) async-start(bf16[16,64,1024]{2,1,0:T(8,128)(2,1)} %gather_fusion.1), calls=%async_computation.2 | async-start | bytes 4194304 | tf_op jit(solution)/shard_map/all_to_all | solution.py:206
  78.6 3.3 %shard_map.68 = bf16[8,64,128]{2,1,0:T(8,128)(2,1)S(1)} custom-call(s32[8]{0:T(128)S(1)} %copy-done.2, bf16[1024,1024]{1,0:T(8,128)(2,1)} %a_ref.9, bf16[16,64,1024]{2,1,0:T(8,128)(2,1)} %all-to-all-done.1.refs_0_.refs_1_.refs_2_.refs_3_.refs_4_.refs_5_.refs_6_.refs_7_, ...), custom_call_target="tpu_custom_call" | custom-call | flops 10000000000 | bytes 10000000 | tf_op jit(solution)/shard_map/pallas_call | solution.py:110
  82.0 0.6 collective-permute-done.3.refs_0_
  82.6 1.5 %collective-permute-start.7 = (bf16[512,1024]{1,0:T(8,128)(2,1)S(1)}, bf16[512,1024]{1,0:T(8,128)(2,1)}, u32[]{:S(2)}, u32[]{:S(2)}) collective-permute-start(bf16[512,1024]{1,0:T(8,128)(2,1)S(1)} %copy-done.5), channel_id=1, source_target_pairs={{0,2},{1,3},{2,4},{3,5},{4,6},{5,7},{6,0},{7,1},{8,10},{9,11},{10,... | collective-permute-start | bytes 3145736 | tf_op jit(solution)/shard_map/ppermute | solution.py:200
  84.1 0.6 collective-permute-start.8
  84.7 2.7 %collective-permute-start.10 = (bf16[8,64,128]{2,1,0:T(8,128)(2,1)S(1)}, bf16[8,64,128]{2,1,0:T(8,128)(2,1)S(1)}, u32[]{:S(2)}, u32[]{:S(2)}) collective-permute-start(bf16[8,64,128]{2,1,0:T(8,128)(2,1)S(1)} %add_convert_fusion.refs_4_), channel_id=1, source_target_pairs={{0,2},{1,3},{2,4},{3,5},{4,6},{5,7},{6,0},{7,1},{8,10},{9,11},{10,... | collective-permute-start | bytes 393224 | tf_op jit(solution)/shard_map/ppermute | solution.py:200
  87.5 0.9 collective-permute-start.12
  88.4 10.3 %shard_map.67 = (bf16[512,1024]{1,0:T(8,128)(2,1)}, bf16[512,1024]{1,0:T(8,128)(2,1)}) custom-call(s32[8]{0:T(128)S(1)} %fusion.1.sched, bf16[1024,1024]{1,0:T(8,128)(2,1)} %a_ref.9, bf16[1024,1024]{1,0:T(8,128)(2,1)} %collective-permute-done.ap_ref, bf16[1024,8192]{1,0:T(8,128)(2,1)} %w_ref.7, bf16[1024,8192]{1,0:T(8,128)(2,1)} %collective-permute-done.2.wp_ref, ...), custom_call_target="tpu_custom_call" | custom-call | flops 10000000000 | bytes 10000000 | tf_op jit(solution)/shard_map/pallas_call | solution.py:80
  98.8 5.6 %all-to-all-done.2.refs_8_.refs_9_.refs_10_.refs_11_.refs_12_.refs_13_.refs_14_.refs_15_ = bf16[16,64,1024]{2,1,0:T(8,128)(2,1)} async-done(((bf16[16,64,1024]{2,1,0:T(8,128)(2,1)}), bf16[16,64,1024]{2,1,0:T(8,128)(2,1)}, u32[]{:S(2)}, u32[]{:S(2)}) %all-to-all-start.2) | async-done | bytes 2097184 | tf_op jit(solution)/shard_map/all_to_all | solution.py:206
  104.4 7.1 %collective-permute-done.10.refs_5_ = bf16[8,64,128]{2,1,0:T(8,128)(2,1)S(1)} collective-permute-done((bf16[8,64,128]{2,1,0:T(8,128)(2,1)S(1)}, bf16[8,64,128]{2,1,0:T(8,128)(2,1)S(1)}, u32[]{:S(2)}, u32[]{:S(2)}) %collective-permute-start.10) | collective-permute-done | bytes 131104 | tf_op jit(solution)/shard_map/ppermute | solution.py:200
  111.5 1.5 %collective-permute-done.11.refs_6_ = bf16[8,64,128]{2,1,0:T(8,128)(2,1)S(1)} collective-permute-done((bf16[8,64,128]{2,1,0:T(8,128)(2,1)S(1)}, bf16[8,64,128]{2,1,0:T(8,128)(2,1)S(1)}, u32[]{:S(2)}, u32[]{:S(2)}) %collective-permute-start.11) | collective-permute-done | bytes 131104 | tf_op jit(solution)/shard_map/ppermute | solution.py:200
  113.0 2.9 %collective-permute-done.12.refs_7_ = bf16[8,64,128]{2,1,0:T(8,128)(2,1)S(1)} collective-permute-done((bf16[8,64,128]{2,1,0:T(8,128)(2,1)S(1)}, bf16[8,64,128]{2,1,0:T(8,128)(2,1)S(1)}, u32[]{:S(2)}, u32[]{:S(2)}) %collective-permute-start.12) | collective-permute-done | bytes 131104 | tf_op jit(solution)/shard_map/ppermute | solution.py:200
  115.8 0.6 copy-done.12
  116.5 6.2 %shard_map.69 = bf16[1024,1024]{1,0:T(8,128)(2,1)} custom-call(s32[8]{0:T(128)S(1)} %copy-done.2, s32[8]{0:T(128)S(1)} %copy-done.3, bf16[512,1024]{1,0:T(8,128)(2,1)} %get-tuple-element.27.refs_0_, bf16[512,1024]{1,0:T(8,128)(2,1)} %collective-permute-done.7.refs_1_, bf16[512,1024]{1,0:T(8,128)(2,1)} %get-tuple-element.28.refs_2_, ...), custom_call_target="tpu_custom_call" | custom-call | flops 10000000000 | bytes 10000000 | tf_op jit(solution)/shard_map/pallas_call | solution.py:167
  (43 shorter events, 1.5 us)
Async XLA Ops:
  0.0 36.7 %copy-start = (bf16[12,64,1024]{2,1,0:T(8,128)(2,1)S(1)}, bf16[12,64,1024]{2,1,0:T(8,128)(2,1)}, u32[]{:S(2)}) copy-start(bf16[12,64,1024]{2,1,0:T(8,128)(2,1)} %param.8) | copy-start | bytes 4718596
  0.0 4.5 %collective-permute-start = (bf16[1024,1024]{1,0:T(8,128)(2,1)}, bf16[1024,1024]{1,0:T(8,128)(2,1)}, u32[]{:S(2)}, u32[]{:S(2)}) collective-permute-start(bf16[1024,1024]{1,0:T(8,128)(2,1)} %a_ref.9), channel_id=1, source_target_pairs={{0,1},{1,0},{2,3},{3,2},{4,5},{5,4},{6,7},{7,6},{8,9},{9,8},{10,11... | collective-permute-start | bytes 6291464 | tf_op jit(solution)/shard_map/ppermute | solution.py:203
  0.0 8.6 %copy-start.2 = (s32[8]{0:T(128)S(1)}, s32[8]{0:T(128)}, u32[]{:S(2)}) copy-start(s32[8]{0:T(128)} %adapters.3) | copy-start | bytes 100
  1.9 5.2 %collective-permute-start.1 = (bf16[1024,1024]{1,0:T(8,128)(2,1)S(1)}, bf16[1024,1024]{1,0:T(8,128)(2,1)S(1)}, u32[]{:S(2)}, u32[]{:S(2)}) collective-permute-start(bf16[1024,1024]{1,0:T(8,128)(2,1)S(1)} %constant_dynamic-slice_fusion), channel_id=1, source_target_pairs={{0,1},{1,0},{2,3},{3,2},{4,5},{5,4},{6,7},{7,6},{8,9},{9,8},{10,11... | collective-permute-start | bytes 6291464 | tf_op jit(solution)/shard_map/ppermute | solution.py:203
  7.2 1.3 %copy-start.9 = (bf16[1024,1024]{1,0:T(8,128)(2,1)}, bf16[1024,1024]{1,0:T(8,128)(2,1)S(1)}, u32[]{:S(2)}) copy-start(bf16[1024,1024]{1,0:T(8,128)(2,1)S(1)} %collective-permute-done.1.wp_ref) | copy-start | bytes 6291460
  8.5 37.8 %collective-permute-start.2 = (bf16[1024,8192]{1,0:T(8,128)(2,1)}, bf16[1024,8192]{1,0:T(8,128)(2,1)}, u32[]{:S(2)}, u32[]{:S(2)}) collective-permute-start(bf16[1024,8192]{1,0:T(8,128)(2,1)} %w_ref.7), channel_id=1, source_target_pairs={{0,1},{1,0},{2,3},{3,2},{4,5},{5,4},{6,7},{7,6},{8,9},{9,8},{10,11... | collective-permute-start | bytes 50331656 | tf_op jit(solution)/shard_map/ppermute | solution.py:203
  9.4 14.6 %all-to-all-start = ((s32[16,1,128]{2,1,0:T(1,128)}), s32[16,1,128]{2,1,0:T(1,128)S(1)}, u32[]{:S(2)}, u32[]{:S(2)}) async-start(s32[16,1,128]{2,1,0:T(1,128)} %broadcast_in_dim.27), calls=%async_computation | async-start | bytes 16384 | tf_op jit(solution)/shard_map/all_to_all | solution.py:206
  24.0 0.6 copy-start.8
  34.6 24.9 %collective-permute-start.5 = (bf16[512,1024]{1,0:T(8,128)(2,1)}, bf16[512,1024]{1,0:T(8,128)(2,1)}, u32[]{:S(2)}, u32[]{:S(2)}) collective-permute-start(bf16[512,1024]{1,0:T(8,128)(2,1)} %get-tuple-element.20.refs_0_), channel_id=1, source_target_pairs={{0,2},{1,3},{2,4},{3,5},{4,6},{5,7},{6,0},{7,1},{8,10},{9,11},{10,... | collective-permute-start | bytes 3145736 | tf_op jit(solution)/shard_map/ppermute | solution.py:200
  35.1 26.5 %collective-permute-start.6 = (bf16[512,1024]{1,0:T(8,128)(2,1)}, bf16[512,1024]{1,0:T(8,128)(2,1)}, u32[]{:S(2)}, u32[]{:S(2)}) collective-permute-start(bf16[512,1024]{1,0:T(8,128)(2,1)} %get-tuple-element.23), channel_id=1, source_target_pairs={{0,6},{1,7},{2,0},{3,1},{4,2},{5,3},{6,4},{7,5},{8,14},{9,15},{10,... | collective-permute-start | bytes 3145736 | tf_op jit(solution)/shard_map/ppermute | solution.py:200
  38.7 5.6 %copy-start.4 = (bf16[12,64,1024]{2,1,0:T(8,128)(2,1)S(1)}, bf16[12,64,1024]{2,1,0:T(8,128)(2,1)}, u32[]{:S(2)}) copy-start(bf16[12,64,1024]{2,1,0:T(8,128)(2,1)} %param.9) | copy-start | bytes 4718596
  38.7 33.3 %all-to-all-start.1 = ((bf16[16,64,1024]{2,1,0:T(8,128)(2,1)}), bf16[16,64,1024]{2,1,0:T(8,128)(2,1)}, u32[]{:S(2)}, u32[]{:S(2)}) async-start(bf16[16,64,1024]{2,1,0:T(8,128)(2,1)} %gather_fusion), calls=%async_computation.1 | async-start | bytes 4194304 | tf_op jit(solution)/shard_map/all_to_all | solution.py:206
  56.3 26.3 %collective-permute-start.3 = (bf16[512,1024]{1,0:T(8,128)(2,1)}, bf16[512,1024]{1,0:T(8,128)(2,1)S(1)}, u32[]{:S(2)}, u32[]{:S(2)}) collective-permute-start(bf16[512,1024]{1,0:T(8,128)(2,1)} %get-tuple-element.21), channel_id=1, source_target_pairs={{0,6},{1,7},{2,0},{3,1},{4,2},{5,3},{6,4},{7,5},{8,14},{9,15},{10,... | collective-permute-start | bytes 3145736 | tf_op jit(solution)/shard_map/ppermute | solution.py:200
  57.1 25.4 %collective-permute-start.4 = (bf16[512,1024]{1,0:T(8,128)(2,1)}, bf16[512,1024]{1,0:T(8,128)(2,1)}, u32[]{:S(2)}, u32[]{:S(2)}) collective-permute-start(bf16[512,1024]{1,0:T(8,128)(2,1)} %get-tuple-element.22.refs_2_), channel_id=1, source_target_pairs={{0,2},{1,3},{2,4},{3,5},{4,6},{5,7},{6,0},{7,1},{8,10},{9,11},{10,... | collective-permute-start | bytes 3145736 | tf_op jit(solution)/shard_map/ppermute | solution.py:200
  72.0 32.4 %all-to-all-start.2 = ((bf16[16,64,1024]{2,1,0:T(8,128)(2,1)}), bf16[16,64,1024]{2,1,0:T(8,128)(2,1)}, u32[]{:S(2)}, u32[]{:S(2)}) async-start(bf16[16,64,1024]{2,1,0:T(8,128)(2,1)} %gather_fusion.1), calls=%async_computation.2 | async-start | bytes 4194304 | tf_op jit(solution)/shard_map/all_to_all | solution.py:206
  78.6 4.0 %copy-start.5 = (bf16[512,1024]{1,0:T(8,128)(2,1)S(1)}, bf16[512,1024]{1,0:T(8,128)(2,1)}, u32[]{:S(2)}) copy-start(bf16[512,1024]{1,0:T(8,128)(2,1)} %get-tuple-element.26.refs_2_.refs_8_) | copy-start | bytes 3145732
  81.9 2.8 %collective-permute-start.9 = (bf16[8,64,128]{2,1,0:T(8,128)(2,1)S(1)}, bf16[8,64,128]{2,1,0:T(8,128)(2,1)S(1)}, u32[]{:S(2)}, u32[]{:S(2)}) collective-permute-start(bf16[8,64,128]{2,1,0:T(8,128)(2,1)S(1)} %shard_map.68), channel_id=1, source_target_pairs={{0,1},{1,0},{2,3},{3,2},{4,5},{5,4},{6,7},{7,6},{8,9},{9,8},{10,11... | collective-permute-start | bytes 393224 | tf_op jit(solution)/shard_map/ppermute | solution.py:203
  82.6 5.9 %copy-start.6 = (bf16[512,1024]{1,0:T(8,128)(2,1)}, bf16[512,1024]{1,0:T(8,128)(2,1)S(1)}, u32[]{:S(2)}) copy-start(bf16[512,1024]{1,0:T(8,128)(2,1)S(1)} %collective-permute-done.3.refs_0_) | copy-start | bytes 3145732
  82.6 33.2 %collective-permute-start.7 = (bf16[512,1024]{1,0:T(8,128)(2,1)S(1)}, bf16[512,1024]{1,0:T(8,128)(2,1)}, u32[]{:S(2)}, u32[]{:S(2)}) collective-permute-start(bf16[512,1024]{1,0:T(8,128)(2,1)S(1)} %copy-done.5), channel_id=1, source_target_pairs={{0,2},{1,3},{2,4},{3,5},{4,6},{5,7},{6,0},{7,1},{8,10},{9,11},{10,... | collective-permute-start | bytes 3145736 | tf_op jit(solution)/shard_map/ppermute | solution.py:200
  84.1 31.7 %collective-permute-start.8 = (bf16[512,1024]{1,0:T(8,128)(2,1)}, bf16[512,1024]{1,0:T(8,128)(2,1)}, u32[]{:S(2)}, u32[]{:S(2)}) collective-permute-start(bf16[512,1024]{1,0:T(8,128)(2,1)} %get-tuple-element.29), channel_id=1, source_target_pairs={{0,6},{1,7},{2,0},{3,1},{4,2},{5,3},{6,4},{7,5},{8,14},{9,15},{10,... | collective-permute-start | bytes 3145736 | tf_op jit(solution)/shard_map/ppermute | solution.py:200
  84.7 14.1 %copy-start.7 = (bf16[8,64,128]{2,1,0:T(8,128)(2,1)}, bf16[8,64,128]{2,1,0:T(8,128)(2,1)S(1)}, u32[]{:S(2)}) copy-start(bf16[8,64,128]{2,1,0:T(8,128)(2,1)S(1)} %add_convert_fusion.refs_4_) | copy-start | bytes 393220
  84.7 31.7 %copy-start.3 = (s32[8]{0:T(128)S(1)}, s32[8]{0:T(128)}, u32[]{:S(2)}) copy-start(s32[8]{0:T(128)} %fill.1) | copy-start | bytes 100
  84.7 26.7 %collective-permute-start.10 = (bf16[8,64,128]{2,1,0:T(8,128)(2,1)S(1)}, bf16[8,64,128]{2,1,0:T(8,128)(2,1)S(1)}, u32[]{:S(2)}, u32[]{:S(2)}) collective-permute-start(bf16[8,64,128]{2,1,0:T(8,128)(2,1)S(1)} %add_convert_fusion.refs_4_), channel_id=1, source_target_pairs={{0,2},{1,3},{2,4},{3,5},{4,6},{5,7},{6,0},{7,1},{8,10},{9,11},{10,... | collective-permute-start | bytes 393224 | tf_op jit(solution)/shard_map/ppermute | solution.py:200
  87.5 25.5 %collective-permute-start.11 = (bf16[8,64,128]{2,1,0:T(8,128)(2,1)S(1)}, bf16[8,64,128]{2,1,0:T(8,128)(2,1)S(1)}, u32[]{:S(2)}, u32[]{:S(2)}) collective-permute-start(bf16[8,64,128]{2,1,0:T(8,128)(2,1)S(1)} %add_convert_fusion.refs_4_), channel_id=1, source_target_pairs={{0,4},{1,5},{2,6},{3,7},{4,0},{5,1},{6,2},{7,3},{8,12},{9,13},{10,... | collective-permute-start | bytes 393224 | tf_op jit(solution)/shard_map/ppermute | solution.py:200
  87.5 28.3 %collective-permute-start.12 = (bf16[8,64,128]{2,1,0:T(8,128)(2,1)S(1)}, bf16[8,64,128]{2,1,0:T(8,128)(2,1)S(1)}, u32[]{:S(2)}, u32[]{:S(2)}) collective-permute-start(bf16[8,64,128]{2,1,0:T(8,128)(2,1)S(1)} %add_convert_fusion.refs_4_), channel_id=1, source_target_pairs={{0,6},{1,7},{2,0},{3,1},{4,2},{5,3},{6,4},{7,5},{8,14},{9,15},{10,... | collective-permute-start | bytes 393224 | tf_op jit(solution)/shard_map/ppermute | solution.py:200
  111.5 4.3 %copy-start.10 = (bf16[8,64,128]{2,1,0:T(8,128)(2,1)}, bf16[8,64,128]{2,1,0:T(8,128)(2,1)S(1)}, u32[]{:S(2)}) copy-start(bf16[8,64,128]{2,1,0:T(8,128)(2,1)S(1)} %collective-permute-done.10.refs_5_) | copy-start | bytes 393220
  112.9 2.9 %copy-start.11 = (bf16[8,64,128]{2,1,0:T(8,128)(2,1)}, bf16[8,64,128]{2,1,0:T(8,128)(2,1)S(1)}, u32[]{:S(2)}) copy-start(bf16[8,64,128]{2,1,0:T(8,128)(2,1)S(1)} %collective-permute-done.11.refs_6_) | copy-start | bytes 393220
  115.8 0.6 copy-start.12
  116.5 6.2 %copy-start.1 = (bf16[12,64,1024]{2,1,0:T(8,128)(2,1)S(1)}, bf16[12,64,1024]{2,1,0:T(8,128)(2,1)}, u32[]{:S(2)}) copy-start(bf16[12,64,1024]{2,1,0:T(8,128)(2,1)} %param.8) | copy-start | bytes 4718596

commit v3 on v2

--- a/solution.py
+++ b/solution.py
@@ -8,6 +8,7 @@
 from jax.sharding import PartitionSpec as P
 
 BN = 512
+FBN = 1024
 IDS = 1
 COST = pl.CostEstimate(flops=10000000000,bytes_accessed=10000000, transcendentals=0)
 
@@ -148,19 +149,19 @@
 def finish(adapters, fill, parts, lows, expand_slots, per_owner):
     blocks = adapters.shape[0]
     rows, width = parts[0].shape
-    steps = width // BN
+    steps = width // FBN
     per = blocks // 2
     rank = expand_slots.shape[1]
     in_specs = []
     for k0 in range(2):
         for _ in range(2):
-            in_specs.append(pl.BlockSpec((rows, BN), lambda k, j, ad, fl, k0=k0: (0, clamp(k * steps + j, steps, k0))))
+            in_specs.append(pl.BlockSpec((rows, FBN), lambda k, j, ad, fl, k0=k0: (0, clamp(k * steps + j, steps, k0))))
     for low in lows:
         in_specs.append(pl.BlockSpec(low.shape, lambda k, j, ad, fl: (0, 0, 0)))
     for b in range(blocks):
         in_specs.append(
             pl.BlockSpec(
-                (1, rank, BN),
+                (1, rank, FBN),
                 lambda k, j, ad, fl, b=b: (ad[b] // per_owner, 0, clamp(k * steps + j, steps, b // per)),
             )
         )
@@ -170,7 +171,7 @@
             num_scalar_prefetch=2,
             grid=(2, steps),
             in_specs=in_specs,
-            out_specs=pl.BlockSpec((rows, BN), lambda k, j, ad, fl: (k, j)),
+            out_specs=pl.BlockSpec((rows, FBN), lambda k, j, ad, fl: (k, j)),
         ),
         out_shape=jax.ShapeDtypeStruct((2 * rows, width), jnp.bfloat16),
         compiler_params=params(),
@@ -219,10 +220,10 @@
     weight_other = swap(after(out_weight, opp_other, att_other))
     mm = functools.partial(matmuls, sched, attended, att_other, out_weight)
 
-    opp_a, opp_b = mm(opp_other, half, [(OPP, 0, ()), (OPP, half, ())], deps=(asked,))
+    opp_a, opp_b = mm(opp_other, half, [(OPP, 0, ()), (OPP, half, ())], deps=())
     right_1, left_1 = send(opp_a, 1), send(opp_b, -1)
 
-    served = after(asked[:, 0, 0], opp_a)
+    served = after(asked, opp_a)[:, 0, 0]
     shrink_slots = exchange(shrink_weight[served])
     expand_slots = exchange(expand_weight[served])
 

time: 123 us -> 121 us (0.984)
  waiting for transfers between devices: 30.7 us -> 24.7 us
  starting transfers between devices: 32.3 us -> 36 us
    all_to_all x3, waiting for transfers between devices: 11.8 us -> 6.88 us  [exchange(): return lax.all_to_all(a, 'replica', 0, 0, tiled=True)]
    all_to_all x3, starting transfers between devices: 20.6 us -> 23.7 us  [exchange(): return lax.all_to_all(a, 'replica', 0, 0, tiled=True)]
    ppermute x9, waiting for transfers between devices: 14.1 us -> 11.2 us  [send(): return lax.ppermute(a, 'tensor', pairs)]
    ppermute x4, waiting for transfers between devices: 4.79 us -> 6.65 us  [swap(): return lax.ppermute(a, 'tensor', [(s, s ^ 1) for s in range(n_tensor)])]
  transfers between devices with their start and end apart: 16 -> 16, of which waited for: 9 -> 7; matrix products, arithmetic and copies ran while one was open for 6% -> 4% of each run, Pallas kernels for 36% -> 37%
where the time goes in v3:
time: 121 us; the launch traced here: 120 us
  Pallas kernels  49.8 us (41%)
  starting transfers between devices  36 us (30%)
  waiting for transfers between devices  24.7 us (20%)
  local copies, waits for them, and re-layouts  9.33 us (8%)
    pallas_call x4, Pallas kernels, matmuls(): pl.pallas_call(functools.partial(tasks_kernel, [len(t[2]) for t in tasks]...  40.7 us
    all_to_all x3, starting transfers between devices, exchange(): return lax.all_to_all(a, 'replica', 0, 0, tiled=True)  23.7 us
    ppermute x9, starting transfers between devices, send(): return lax.ppermute(a, 'tensor', pairs)  11.8 us
    ppermute x9, waiting for transfers between devices, send(): return lax.ppermute(a, 'tensor', pairs)  11.2 us
    all_to_all x3, waiting for transfers between devices, exchange(): return lax.all_to_all(a, 'replica', 0, 0, tiled=True)  6.88 us
    ppermute x4, waiting for transfers between devices, swap(): return lax.ppermute(a, 'tensor', [(s, s ^ 1) for s in range(n_tensor)])  6.65 us
    pallas_call x1, Pallas kernels, finish(): pl.pallas_call(functools.partial(final_kernel, per, len(lows)), grid_spec...  5.76 us
    pallas_call x1, Pallas kernels, shrink(): pl.pallas_call(functools.partial(shrink_kernel, blocks, rows), grid_spec=...  3.29 us
  transfers between devices with their start and end apart: 16, of which 7 were waited for; matrix products, arithmetic and copies ran while one was open for 4% of the time, Pallas kernels for 37%

profile of v3, /device:TPU:14, one launch (start us, length us, event | category | flops | bytes accessed | tf_op | source)
XLA Modules:
  0.0 120.4 jit_solution(11437267156400407939)
XLA Ops:
  0.0 1.9 %constant_dynamic-slice_fusion = bf16[1024,1024]{1,0:T(8,128)(2,1)S(1)} fusion(bf16[1024,8192]{1,0:T(8,128)(2,1)} %w_ref.7, s32[]{:T(128)S(6)} %select_n.31), kind=kLoop, calls=%fused_computation.17 | loop fusion | bytes 4194308 | tf_op jit(solution)/shard_map/dynamic_slice | solution.py:217
  2.0 0.3 copy-done.4
  2.4 0.2 collective-permute-start
  2.5 3.6 %collective-permute-done.1.wp_ref = bf16[1024,1024]{1,0:T(8,128)(2,1)S(1)} collective-permute-done((bf16[1024,1024]{1,0:T(8,128)(2,1)S(1)}, bf16[1024,1024]{1,0:T(8,128)(2,1)S(1)}, u32[]{:S(2)}, u32[]{:S(2)}) %collective-permute-start.1) | collective-permute-done | bytes 2097184 | tf_op jit(solution)/shard_map/ppermute | solution.py:204
  6.2 3.0 %collective-permute-done.ap_ref = bf16[1024,1024]{1,0:T(8,128)(2,1)S(1)} collective-permute-done((bf16[1024,1024]{1,0:T(8,128)(2,1)S(1)}, bf16[1024,1024]{1,0:T(8,128)(2,1)S(1)}, u32[]{:S(2)}, u32[]{:S(2)}) %collective-permute-start) | collective-permute-done | bytes 2097184 | tf_op jit(solution)/shard_map/ppermute | solution.py:204
  9.2 1.3 %copy-done.5 = bf16[1024,1024]{1,0:T(8,128)(2,1)} copy-done((bf16[1024,1024]{1,0:T(8,128)(2,1)}, bf16[1024,1024]{1,0:T(8,128)(2,1)S(1)}, u32[]{:S(2)}) %copy-start.5) | copy-done | bytes 2097176
  10.7 0.7 broadcast_in_dim.16
  11.4 8.4 %all-to-all-start = ((s32[16,1,128]{2,1,0:T(1,128)}), s32[16,1,128]{2,1,0:T(1,128)S(1)}, u32[]{:S(2)}, u32[]{:S(2)}) async-start(s32[16,1,128]{2,1,0:T(1,128)} %broadcast_in_dim.16), calls=%async_computation | async-start | bytes 16384 | tf_op jit(solution)/shard_map/all_to_all | solution.py:207
  19.9 10.0 %shard_map.64 = (bf16[512,1024]{1,0:T(8,128)(2,1)}, bf16[512,1024]{1,0:T(8,128)(2,1)}) custom-call(s32[8]{0:T(128)S(1)} %fusion.1.sched, bf16[1024,1024]{1,0:T(8,128)(2,1)} %a_ref.9, bf16[1024,1024]{1,0:T(8,128)(2,1)} %copy-done.5, bf16[1024,8192]{1,0:T(8,128)(2,1)} %w_ref.7, bf16[1024,1024]{1,0:T(8,128)(2,1)} %copy-done.10), custom_call_target="tpu_custom_call" | custom-call | flops 10000000000 | bytes 10000000 | tf_op jit(solution)/shard_map/pallas_call | solution.py:81
  29.9 0.5 collective-permute-start.5
  30.4 1.5 %collective-permute-start.6 = (bf16[512,1024]{1,0:T(8,128)(2,1)}, bf16[512,1024]{1,0:T(8,128)(2,1)}, u32[]{:S(2)}, u32[]{:S(2)}) collective-permute-start(bf16[512,1024]{1,0:T(8,128)(2,1)} %get-tuple-element.22), channel_id=1, source_target_pairs={{0,6},{1,7},{2,0},{3,1},{4,2},{5,3},{6,4},{7,5},{8,14},{9,15},{10,... | collective-permute-start | bytes 3145736 | tf_op jit(solution)/shard_map/ppermute | solution.py:201
  31.9 0.4 slice_reduce_fusion
  32.3 2.0 %gather_fusion = bf16[16,64,1024]{2,1,0:T(8,128)(2,1)} fusion(bf16[12,64,1024]{2,1,0:T(8,128)(2,1)S(1)} %copy-done, s32[1024]{0:T(1024)S(1)} %pad_clamp_fusion), kind=kCustom, calls=%fused_computation | custom fusion | bytes 4194368 | tf_op jit(solution)/shard_map/gather | solution.py:227
  34.3 7.4 %all-to-all-start.1 = ((bf16[16,64,1024]{2,1,0:T(8,128)(2,1)}), bf16[16,64,1024]{2,1,0:T(8,128)(2,1)}, u32[]{:S(2)}, u32[]{:S(2)}) async-start(bf16[16,64,1024]{2,1,0:T(8,128)(2,1)} %gather_fusion), calls=%async_computation.1 | async-start | bytes 4194304 | tf_op jit(solution)/shard_map/all_to_all | solution.py:207
  41.7 2.0 %gather_fusion.1 = bf16[16,64,1024]{2,1,0:T(8,128)(2,1)} fusion(bf16[12,64,1024]{2,1,0:T(8,128)(2,1)S(1)} %copy-done.6, s32[1024]{0:T(1024)S(1)} %pad_clamp_fusion), kind=kCustom, calls=%fused_computation.1 | custom fusion | bytes 4194368 | tf_op jit(solution)/shard_map/gather | solution.py:228
  43.7 10.0 %shard_map.65 = (bf16[512,1024]{1,0:T(8,128)(2,1)}, bf16[512,1024]{1,0:T(8,128)(2,1)}) custom-call(s32[8]{0:T(128)S(1)} %fusion.1.sched, bf16[1024,1024]{1,0:T(8,128)(2,1)} %a_ref.9, bf16[1024,1024]{1,0:T(8,128)(2,1)} %copy-done.5, bf16[1024,8192]{1,0:T(8,128)(2,1)} %w_ref.7, bf16[1024,8192]{1,0:T(8,128)(2,1)} %collective-permute-done.2.wp_ref, ...), custom_call_target="tpu_custom_call" | custom-call | flops 10000000000 | bytes 10000000 | tf_op jit(solution)/shard_map/pallas_call | solution.py:81
  53.8 0.8 collective-permute-start.3
  54.6 2.4 %collective-permute-start.4 = (bf16[512,1024]{1,0:T(8,128)(2,1)}, bf16[512,1024]{1,0:T(8,128)(2,1)}, u32[]{:S(2)}, u32[]{:S(2)}) collective-permute-start(bf16[512,1024]{1,0:T(8,128)(2,1)} %get-tuple-element.21.refs_2_), channel_id=1, source_target_pairs={{0,2},{1,3},{2,4},{3,5},{4,6},{5,7},{6,0},{7,1},{8,10},{9,11},{10,... | collective-permute-start | bytes 3145736 | tf_op jit(solution)/shard_map/ppermute | solution.py:201
  57.0 10.3 %shard_map.66 = (bf16[512,1024]{1,0:T(8,128)(2,1)}, bf16[512,1024]{1,0:T(8,128)(2,1)}) custom-call(s32[8]{0:T(128)S(1)} %fusion.1.sched, bf16[1024,1024]{1,0:T(8,128)(2,1)} %a_ref.9, bf16[1024,1024]{1,0:T(8,128)(2,1)} %copy-done.5, bf16[1024,8192]{1,0:T(8,128)(2,1)} %w_ref.7, bf16[1024,8192]{1,0:T(8,128)(2,1)} %collective-permute-done.2.wp_ref, ...), custom_call_target="tpu_custom_call" | custom-call | flops 10000000000 | bytes 10000000 | tf_op jit(solution)/shard_map/pallas_call | solution.py:81
  67.3 1.0 all-to-all-done.1.refs_0_.refs_1_.refs_2_.refs_3_.refs_4_.refs_5_.refs_6_.refs_7_
  68.3 8.0 %all-to-all-start.2 = ((bf16[16,64,1024]{2,1,0:T(8,128)(2,1)}), bf16[16,64,1024]{2,1,0:T(8,128)(2,1)}, u32[]{:S(2)}, u32[]{:S(2)}) async-start(bf16[16,64,1024]{2,1,0:T(8,128)(2,1)} %gather_fusion.1), calls=%async_computation.2 | async-start | bytes 4194304 | tf_op jit(solution)/shard_map/all_to_all | solution.py:207
  76.3 3.3 %shard_map.68 = bf16[8,64,128]{2,1,0:T(8,128)(2,1)S(1)} custom-call(s32[8]{0:T(128)S(1)} %copy-done.2, bf16[1024,1024]{1,0:T(8,128)(2,1)} %a_ref.9, bf16[16,64,1024]{2,1,0:T(8,128)(2,1)} %all-to-all-done.1.refs_0_.refs_1_.refs_2_.refs_3_.refs_4_.refs_5_.refs_6_.refs_7_, ...), custom_call_target="tpu_custom_call" | custom-call | flops 10000000000 | bytes 10000000 | tf_op jit(solution)/shard_map/pallas_call | solution.py:111
  79.7 2.3 %collective-permute-start.7 = (bf16[512,1024]{1,0:T(8,128)(2,1)S(1)}, bf16[512,1024]{1,0:T(8,128)(2,1)}, u32[]{:S(2)}, u32[]{:S(2)}) collective-permute-start(bf16[512,1024]{1,0:T(8,128)(2,1)S(1)} %copy-done.7), channel_id=1, source_target_pairs={{0,2},{1,3},{2,4},{3,5},{4,6},{5,7},{6,0},{7,1},{8,10},{9,11},{10,... | collective-permute-start | bytes 3145736 | tf_op jit(solution)/shard_map/ppermute | solution.py:201
  82.1 3.3 %collective-permute-start.10 = (bf16[8,64,128]{2,1,0:T(8,128)(2,1)S(1)}, bf16[8,64,128]{2,1,0:T(8,128)(2,1)S(1)}, u32[]{:S(2)}, u32[]{:S(2)}) collective-permute-start(bf16[8,64,128]{2,1,0:T(8,128)(2,1)S(1)} %add_convert_fusion.refs_4_), channel_id=1, source_target_pairs={{0,2},{1,3},{2,4},{3,5},{4,6},{5,7},{6,0},{7,1},{8,10},{9,11},{10,... | collective-permute-start | bytes 393224 | tf_op jit(solution)/shard_map/ppermute | solution.py:201
  85.4 0.9 collective-permute-start.12
  86.3 10.3 %shard_map.67 = (bf16[512,1024]{1,0:T(8,128)(2,1)}, bf16[512,1024]{1,0:T(8,128)(2,1)}) custom-call(s32[8]{0:T(128)S(1)} %fusion.1.sched, bf16[1024,1024]{1,0:T(8,128)(2,1)} %a_ref.9, bf16[1024,1024]{1,0:T(8,128)(2,1)} %copy-done.5, bf16[1024,8192]{1,0:T(8,128)(2,1)} %w_ref.7, bf16[1024,8192]{1,0:T(8,128)(2,1)} %collective-permute-done.2.wp_ref, ...), custom_call_target="tpu_custom_call" | custom-call | flops 10000000000 | bytes 10000000 | tf_op jit(solution)/shard_map/pallas_call | solution.py:81
  96.7 5.9 %all-to-all-done.2.refs_8_.refs_9_.refs_10_.refs_11_.refs_12_.refs_13_.refs_14_.refs_15_ = bf16[16,64,1024]{2,1,0:T(8,128)(2,1)} async-done(((bf16[16,64,1024]{2,1,0:T(8,128)(2,1)}), bf16[16,64,1024]{2,1,0:T(8,128)(2,1)}, u32[]{:S(2)}, u32[]{:S(2)}) %all-to-all-start.2) | async-done | bytes 2097184 | tf_op jit(solution)/shard_map/all_to_all | solution.py:207
  102.6 6.0 %collective-permute-done.10.refs_5_ = bf16[8,64,128]{2,1,0:T(8,128)(2,1)S(1)} collective-permute-done((bf16[8,64,128]{2,1,0:T(8,128)(2,1)S(1)}, bf16[8,64,128]{2,1,0:T(8,128)(2,1)S(1)}, u32[]{:S(2)}, u32[]{:S(2)}) %collective-permute-start.10) | collective-permute-done | bytes 131104 | tf_op jit(solution)/shard_map/ppermute | solution.py:201
  108.6 2.0 %collective-permute-done.11.refs_6_ = bf16[8,64,128]{2,1,0:T(8,128)(2,1)S(1)} collective-permute-done((bf16[8,64,128]{2,1,0:T(8,128)(2,1)S(1)}, bf16[8,64,128]{2,1,0:T(8,128)(2,1)S(1)}, u32[]{:S(2)}, u32[]{:S(2)}) %collective-permute-start.11) | collective-permute-done | bytes 131104 | tf_op jit(solution)/shard_map/ppermute | solution.py:201
  110.5 3.3 %collective-permute-done.12.refs_7_ = bf16[8,64,128]{2,1,0:T(8,128)(2,1)S(1)} collective-permute-done((bf16[8,64,128]{2,1,0:T(8,128)(2,1)S(1)}, bf16[8,64,128]{2,1,0:T(8,128)(2,1)S(1)}, u32[]{:S(2)}, u32[]{:S(2)}) %collective-permute-start.12) | collective-permute-done | bytes 131104 | tf_op jit(solution)/shard_map/ppermute | solution.py:201
  113.8 0.6 copy-done.13
  114.4 5.8 %shard_map.69 = bf16[1024,1024]{1,0:T(8,128)(2,1)} custom-call(s32[8]{0:T(128)S(1)} %copy-done.2, s32[8]{0:T(128)S(1)} %copy-done.3, bf16[512,1024]{1,0:T(8,128)(2,1)} %get-tuple-element.26.refs_0_, bf16[512,1024]{1,0:T(8,128)(2,1)} %collective-permute-done.7.refs_1_, bf16[512,1024]{1,0:T(8,128)(2,1)} %get-tuple-element.27.refs_2_, ...), custom_call_target="tpu_custom_call" | custom-call | flops 10000000000 | bytes 10000000 | tf_op jit(solution)/shard_map/pallas_call | solution.py:168
  (45 shorter events, 0.6 us)
Async XLA Ops:
  0.0 32.3 %copy-start = (bf16[12,64,1024]{2,1,0:T(8,128)(2,1)S(1)}, bf16[12,64,1024]{2,1,0:T(8,128)(2,1)}, u32[]{:S(2)}) copy-start(bf16[12,64,1024]{2,1,0:T(8,128)(2,1)} %param.8) | copy-start | bytes 4718596
  0.0 2.3 %copy-start.4 = (bf16[1024,1024]{1,0:T(8,128)(2,1)S(1)}, bf16[1024,1024]{1,0:T(8,128)(2,1)}, u32[]{:S(2)}) copy-start(bf16[1024,1024]{1,0:T(8,128)(2,1)} %a_ref.9) | copy-start | bytes 6291460
  0.0 10.6 %copy-start.2 = (s32[8]{0:T(128)S(1)}, s32[8]{0:T(128)}, u32[]{:S(2)}) copy-start(s32[8]{0:T(128)} %adapters.3) | copy-start | bytes 100
  1.9 4.2 %collective-permute-start.1 = (bf16[1024,1024]{1,0:T(8,128)(2,1)S(1)}, bf16[1024,1024]{1,0:T(8,128)(2,1)S(1)}, u32[]{:S(2)}, u32[]{:S(2)}) collective-permute-start(bf16[1024,1024]{1,0:T(8,128)(2,1)S(1)} %constant_dynamic-slice_fusion), channel_id=1, source_target_pairs={{0,1},{1,0},{2,3},{3,2},{4,5},{5,4},{6,7},{7,6},{8,9},{9,8},{10,11... | collective-permute-start | bytes 6291464 | tf_op jit(solution)/shard_map/ppermute | solution.py:204
  2.4 6.8 %collective-permute-start = (bf16[1024,1024]{1,0:T(8,128)(2,1)S(1)}, bf16[1024,1024]{1,0:T(8,128)(2,1)S(1)}, u32[]{:S(2)}, u32[]{:S(2)}) collective-permute-start(bf16[1024,1024]{1,0:T(8,128)(2,1)S(1)} %copy-done.4), channel_id=1, source_target_pairs={{0,1},{1,0},{2,3},{3,2},{4,5},{5,4},{6,7},{7,6},{8,9},{9,8},{10,11... | collective-permute-start | bytes 6291464 | tf_op jit(solution)/shard_map/ppermute | solution.py:204
  6.2 3.0 %copy-start.10 = (bf16[1024,1024]{1,0:T(8,128)(2,1)}, bf16[1024,1024]{1,0:T(8,128)(2,1)S(1)}, u32[]{:S(2)}) copy-start(bf16[1024,1024]{1,0:T(8,128)(2,1)S(1)} %collective-permute-done.1.wp_ref) | copy-start | bytes 6291460
  9.2 1.3 %copy-start.5 = (bf16[1024,1024]{1,0:T(8,128)(2,1)}, bf16[1024,1024]{1,0:T(8,128)(2,1)S(1)}, u32[]{:S(2)}) copy-start(bf16[1024,1024]{1,0:T(8,128)(2,1)S(1)} %collective-permute-done.ap_ref) | copy-start | bytes 6291460
  10.5 33.2 %collective-permute-start.2 = (bf16[1024,8192]{1,0:T(8,128)(2,1)}, bf16[1024,8192]{1,0:T(8,128)(2,1)}, u32[]{:S(2)}, u32[]{:S(2)}) collective-permute-start(bf16[1024,8192]{1,0:T(8,128)(2,1)} %w_ref.7), channel_id=1, source_target_pairs={{0,1},{1,0},{2,3},{3,2},{4,5},{5,4},{6,7},{7,6},{8,9},{9,8},{10,11... | collective-permute-start | bytes 50331656 | tf_op jit(solution)/shard_map/ppermute | solution.py:204
  11.4 20.5 %all-to-all-start = ((s32[16,1,128]{2,1,0:T(1,128)}), s32[16,1,128]{2,1,0:T(1,128)S(1)}, u32[]{:S(2)}, u32[]{:S(2)}) async-start(s32[16,1,128]{2,1,0:T(1,128)} %broadcast_in_dim.16), calls=%async_computation | async-start | bytes 16384 | tf_op jit(solution)/shard_map/all_to_all | solution.py:207
  29.9 27.1 %collective-permute-start.5 = (bf16[512,1024]{1,0:T(8,128)(2,1)}, bf16[512,1024]{1,0:T(8,128)(2,1)}, u32[]{:S(2)}, u32[]{:S(2)}) collective-permute-start(bf16[512,1024]{1,0:T(8,128)(2,1)} %get-tuple-element.19.refs_0_), channel_id=1, source_target_pairs={{0,2},{1,3},{2,4},{3,5},{4,6},{5,7},{6,0},{7,1},{8,10},{9,11},{10,... | collective-permute-start | bytes 3145736 | tf_op jit(solution)/shard_map/ppermute | solution.py:201
  30.4 26.7 %collective-permute-start.6 = (bf16[512,1024]{1,0:T(8,128)(2,1)}, bf16[512,1024]{1,0:T(8,128)(2,1)}, u32[]{:S(2)}, u32[]{:S(2)}) collective-permute-start(bf16[512,1024]{1,0:T(8,128)(2,1)} %get-tuple-element.22), channel_id=1, source_target_pairs={{0,6},{1,7},{2,0},{3,1},{4,2},{5,3},{6,4},{7,5},{8,14},{9,15},{10,... | collective-permute-start | bytes 3145736 | tf_op jit(solution)/shard_map/ppermute | solution.py:201
  34.3 7.4 %copy-start.6 = (bf16[12,64,1024]{2,1,0:T(8,128)(2,1)S(1)}, bf16[12,64,1024]{2,1,0:T(8,128)(2,1)}, u32[]{:S(2)}) copy-start(bf16[12,64,1024]{2,1,0:T(8,128)(2,1)} %param.9) | copy-start | bytes 4718596
  34.3 34.0 %all-to-all-start.1 = ((bf16[16,64,1024]{2,1,0:T(8,128)(2,1)}), bf16[16,64,1024]{2,1,0:T(8,128)(2,1)}, u32[]{:S(2)}, u32[]{:S(2)}) async-start(bf16[16,64,1024]{2,1,0:T(8,128)(2,1)} %gather_fusion), calls=%async_computation.1 | async-start | bytes 4194304 | tf_op jit(solution)/shard_map/all_to_all | solution.py:207
  53.8 25.9 %collective-permute-start.3 = (bf16[512,1024]{1,0:T(8,128)(2,1)}, bf16[512,1024]{1,0:T(8,128)(2,1)S(1)}, u32[]{:S(2)}, u32[]{:S(2)}) collective-permute-start(bf16[512,1024]{1,0:T(8,128)(2,1)} %get-tuple-element.20), channel_id=1, source_target_pairs={{0,6},{1,7},{2,0},{3,1},{4,2},{5,3},{6,4},{7,5},{8,14},{9,15},{10,... | collective-permute-start | bytes 3145736 | tf_op jit(solution)/shard_map/ppermute | solution.py:201
  54.6 25.1 %collective-permute-start.4 = (bf16[512,1024]{1,0:T(8,128)(2,1)}, bf16[512,1024]{1,0:T(8,128)(2,1)}, u32[]{:S(2)}, u32[]{:S(2)}) collective-permute-start(bf16[512,1024]{1,0:T(8,128)(2,1)} %get-tuple-element.21.refs_2_), channel_id=1, source_target_pairs={{0,2},{1,3},{2,4},{3,5},{4,6},{5,7},{6,0},{7,1},{8,10},{9,11},{10,... | collective-permute-start | bytes 3145736 | tf_op jit(solution)/shard_map/ppermute | solution.py:201
  68.3 34.3 %all-to-all-start.2 = ((bf16[16,64,1024]{2,1,0:T(8,128)(2,1)}), bf16[16,64,1024]{2,1,0:T(8,128)(2,1)}, u32[]{:S(2)}, u32[]{:S(2)}) async-start(bf16[16,64,1024]{2,1,0:T(8,128)(2,1)} %gather_fusion.1), calls=%async_computation.2 | async-start | bytes 4194304 | tf_op jit(solution)/shard_map/all_to_all | solution.py:207
  76.3 3.4 %copy-start.7 = (bf16[512,1024]{1,0:T(8,128)(2,1)S(1)}, bf16[512,1024]{1,0:T(8,128)(2,1)}, u32[]{:S(2)}) copy-start(bf16[512,1024]{1,0:T(8,128)(2,1)} %get-tuple-element.25.refs_2_.refs_8_) | copy-start | bytes 3145732
  79.6 2.4 %collective-permute-start.9 = (bf16[8,64,128]{2,1,0:T(8,128)(2,1)S(1)}, bf16[8,64,128]{2,1,0:T(8,128)(2,1)S(1)}, u32[]{:S(2)}, u32[]{:S(2)}) collective-permute-start(bf16[8,64,128]{2,1,0:T(8,128)(2,1)S(1)} %shard_map.68), channel_id=1, source_target_pairs={{0,1},{1,0},{2,3},{3,2},{4,5},{5,4},{6,7},{7,6},{8,9},{9,8},{10,11... | collective-permute-start | bytes 393224 | tf_op jit(solution)/shard_map/ppermute | solution.py:204
  79.7 6.6 %copy-start.8 = (bf16[512,1024]{1,0:T(8,128)(2,1)}, bf16[512,1024]{1,0:T(8,128)(2,1)S(1)}, u32[]{:S(2)}) copy-start(bf16[512,1024]{1,0:T(8,128)(2,1)S(1)} %collective-permute-done.3.refs_0_) | copy-start | bytes 3145732
  79.7 34.1 %collective-permute-start.7 = (bf16[512,1024]{1,0:T(8,128)(2,1)S(1)}, bf16[512,1024]{1,0:T(8,128)(2,1)}, u32[]{:S(2)}, u32[]{:S(2)}) collective-permute-start(bf16[512,1024]{1,0:T(8,128)(2,1)S(1)} %copy-done.7), channel_id=1, source_target_pairs={{0,2},{1,3},{2,4},{3,5},{4,6},{5,7},{6,0},{7,1},{8,10},{9,11},{10,... | collective-permute-start | bytes 3145736 | tf_op jit(solution)/shard_map/ppermute | solution.py:201
  82.0 31.8 %collective-permute-start.8 = (bf16[512,1024]{1,0:T(8,128)(2,1)}, bf16[512,1024]{1,0:T(8,128)(2,1)}, u32[]{:S(2)}, u32[]{:S(2)}) collective-permute-start(bf16[512,1024]{1,0:T(8,128)(2,1)} %get-tuple-element.28), channel_id=1, source_target_pairs={{0,6},{1,7},{2,0},{3,1},{4,2},{5,3},{6,4},{7,5},{8,14},{9,15},{10,... | collective-permute-start | bytes 3145736 | tf_op jit(solution)/shard_map/ppermute | solution.py:201
  82.1 14.6 %copy-start.9 = (bf16[8,64,128]{2,1,0:T(8,128)(2,1)}, bf16[8,64,128]{2,1,0:T(8,128)(2,1)S(1)}, u32[]{:S(2)}) copy-start(bf16[8,64,128]{2,1,0:T(8,128)(2,1)S(1)} %add_convert_fusion.refs_4_) | copy-start | bytes 393220
  82.1 32.4 %copy-start.3 = (s32[8]{0:T(128)S(1)}, s32[8]{0:T(128)}, u32[]{:S(2)}) copy-start(s32[8]{0:T(128)} %fill.1) | copy-start | bytes 100
  82.1 26.5 %collective-permute-start.10 = (bf16[8,64,128]{2,1,0:T(8,128)(2,1)S(1)}, bf16[8,64,128]{2,1,0:T(8,128)(2,1)S(1)}, u32[]{:S(2)}, u32[]{:S(2)}) collective-permute-start(bf16[8,64,128]{2,1,0:T(8,128)(2,1)S(1)} %add_convert_fusion.refs_4_), channel_id=1, source_target_pairs={{0,2},{1,3},{2,4},{3,5},{4,6},{5,7},{6,0},{7,1},{8,10},{9,11},{10,... | collective-permute-start | bytes 393224 | tf_op jit(solution)/shard_map/ppermute | solution.py:201
  85.4 25.1 %collective-permute-start.11 = (bf16[8,64,128]{2,1,0:T(8,128)(2,1)S(1)}, bf16[8,64,128]{2,1,0:T(8,128)(2,1)S(1)}, u32[]{:S(2)}, u32[]{:S(2)}) collective-permute-start(bf16[8,64,128]{2,1,0:T(8,128)(2,1)S(1)} %add_convert_fusion.refs_4_), channel_id=1, source_target_pairs={{0,4},{1,5},{2,6},{3,7},{4,0},{5,1},{6,2},{7,3},{8,12},{9,13},{10,... | collective-permute-start | bytes 393224 | tf_op jit(solution)/shard_map/ppermute | solution.py:201
  85.4 28.4 %collective-permute-start.12 = (bf16[8,64,128]{2,1,0:T(8,128)(2,1)S(1)}, bf16[8,64,128]{2,1,0:T(8,128)(2,1)S(1)}, u32[]{:S(2)}, u32[]{:S(2)}) collective-permute-start(bf16[8,64,128]{2,1,0:T(8,128)(2,1)S(1)} %add_convert_fusion.refs_4_), channel_id=1, source_target_pairs={{0,6},{1,7},{2,0},{3,1},{4,2},{5,3},{6,4},{7,5},{8,14},{9,15},{10,... | collective-permute-start | bytes 393224 | tf_op jit(solution)/shard_map/ppermute | solution.py:201
  108.6 5.2 %copy-start.11 = (bf16[8,64,128]{2,1,0:T(8,128)(2,1)}, bf16[8,64,128]{2,1,0:T(8,128)(2,1)S(1)}, u32[]{:S(2)}) copy-start(bf16[8,64,128]{2,1,0:T(8,128)(2,1)S(1)} %collective-permute-done.10.refs_5_) | copy-start | bytes 393220
  110.5 3.3 %copy-start.12 = (bf16[8,64,128]{2,1,0:T(8,128)(2,1)}, bf16[8,64,128]{2,1,0:T(8,128)(2,1)S(1)}, u32[]{:S(2)}) copy-start(bf16[8,64,128]{2,1,0:T(8,128)(2,1)S(1)} %collective-permute-done.11.refs_6_) | copy-start | bytes 393220
  113.8 0.6 copy-start.13
  114.4 5.8 %copy-start.1 = (bf16[12,64,1024]{2,1,0:T(8,128)(2,1)S(1)}, bf16[12,64,1024]{2,1,0:T(8,128)(2,1)}, u32[]{:S(2)}) copy-start(bf16[12,64,1024]{2,1,0:T(8,128)(2,1)} %param.8) | copy-start | bytes 4718596

commit v4 on v3

--- a/solution.py
+++ b/solution.py
@@ -236,7 +236,7 @@
     chip = (part.astype(jnp.float32) + swap(part).astype(jnp.float32)).astype(jnp.bfloat16)
     lows = [chip] + [send(chip, k) for k in range(1, chips)]
 
-    next_a, prev_b, _, _ = lax.optimization_barrier((next_a, prev_b, right_2, left_2))
+
     right_3, left_3 = send(next_a, 1), send(prev_b, -1)
 
     own_a, own_b = mm([(OWN, 0, ((left_2, 0),)), (OWN, half, ((right_2, 0),))], deps=(next_a,))

time: 121 us -> 121 us (level)
  no operation moved by 1% of the time
where the time goes in v4:
time: 121 us; the launch traced here: 120 us
  Pallas kernels  49.7 us (41%)
  starting transfers between devices  35.5 us (29%)
  waiting for transfers between devices  25.2 us (21%)
  local copies, waits for them, and re-layouts  9.36 us (8%)
    pallas_call x4, Pallas kernels, matmuls(): pl.pallas_call(functools.partial(tasks_kernel, [len(t[2]) for t in tasks]...  40.7 us
    all_to_all x3, starting transfers between devices, exchange(): return lax.all_to_all(a, 'replica', 0, 0, tiled=True)  23.7 us
    ppermute x9, starting transfers between devices, send(): return lax.ppermute(a, 'tensor', pairs)  11.3 us
    ppermute x9, waiting for transfers between devices, send(): return lax.ppermute(a, 'tensor', pairs)  11.1 us
    all_to_all x3, waiting for transfers between devices, exchange(): return lax.all_to_all(a, 'replica', 0, 0, tiled=True)  7.41 us
    ppermute x4, waiting for transfers between devices, swap(): return lax.ppermute(a, 'tensor', [(s, s ^ 1) for s in range(n_tensor)])  6.65 us
    pallas_call x1, Pallas kernels, finish(): pl.pallas_call(functools.partial(final_kernel, per, len(lows)), grid_spec...  5.74 us
    pallas_call x1, Pallas kernels, shrink(): pl.pallas_call(functools.partial(shrink_kernel, blocks, rows), grid_spec=...  3.29 us
  transfers between devices with their start and end apart: 16, of which 7 were waited for; matrix products, arithmetic and copies ran while one was open for 4% of the time, Pallas kernels for 37%

profile of v4, /device:TPU:14, one launch (start us, length us, event | category | flops | bytes accessed | tf_op | source)
XLA Modules:
  0.0 120.3 jit_solution(8619084882261447736)
XLA Ops:
  0.0 1.9 %constant_dynamic-slice_fusion = bf16[1024,1024]{1,0:T(8,128)(2,1)S(1)} fusion(bf16[1024,8192]{1,0:T(8,128)(2,1)} %w_ref.7, s32[]{:T(128)S(6)} %select_n.31), kind=kLoop, calls=%fused_computation.17 | loop fusion | bytes 4194308 | tf_op jit(solution)/shard_map/dynamic_slice | solution.py:217
  2.0 0.3 copy-done.4
  2.5 3.6 %collective-permute-done.1.wp_ref = bf16[1024,1024]{1,0:T(8,128)(2,1)S(1)} collective-permute-done((bf16[1024,1024]{1,0:T(8,128)(2,1)S(1)}, bf16[1024,1024]{1,0:T(8,128)(2,1)S(1)}, u32[]{:S(2)}, u32[]{:S(2)}) %collective-permute-start.1) | collective-permute-done | bytes 2097184 | tf_op jit(solution)/shard_map/ppermute | solution.py:204
  6.2 3.0 %collective-permute-done.ap_ref = bf16[1024,1024]{1,0:T(8,128)(2,1)S(1)} collective-permute-done((bf16[1024,1024]{1,0:T(8,128)(2,1)S(1)}, bf16[1024,1024]{1,0:T(8,128)(2,1)S(1)}, u32[]{:S(2)}, u32[]{:S(2)}) %collective-permute-start) | collective-permute-done | bytes 2097184 | tf_op jit(solution)/shard_map/ppermute | solution.py:204
  9.2 1.3 %copy-done.5 = bf16[1024,1024]{1,0:T(8,128)(2,1)} copy-done((bf16[1024,1024]{1,0:T(8,128)(2,1)}, bf16[1024,1024]{1,0:T(8,128)(2,1)S(1)}, u32[]{:S(2)}) %copy-start.5) | copy-done | bytes 2097176
  10.7 0.7 broadcast_in_dim.16
  11.4 8.4 %all-to-all-start = ((s32[16,1,128]{2,1,0:T(1,128)}), s32[16,1,128]{2,1,0:T(1,128)S(1)}, u32[]{:S(2)}, u32[]{:S(2)}) async-start(s32[16,1,128]{2,1,0:T(1,128)} %broadcast_in_dim.16), calls=%async_computation | async-start | bytes 16384 | tf_op jit(solution)/shard_map/all_to_all | solution.py:207
  19.9 10.0 %shard_map.64 = (bf16[512,1024]{1,0:T(8,128)(2,1)}, bf16[512,1024]{1,0:T(8,128)(2,1)}) custom-call(s32[8]{0:T(128)S(1)} %fusion.1.sched, bf16[1024,1024]{1,0:T(8,128)(2,1)} %a_ref.9, bf16[1024,1024]{1,0:T(8,128)(2,1)} %copy-done.5, bf16[1024,8192]{1,0:T(8,128)(2,1)} %w_ref.7, bf16[1024,1024]{1,0:T(8,128)(2,1)} %copy-done.10), custom_call_target="tpu_custom_call" | custom-call | flops 10000000000 | bytes 10000000 | tf_op jit(solution)/shard_map/pallas_call | solution.py:81
  29.9 0.5 collective-permute-start.5
  30.4 1.5 %collective-permute-start.6 = (bf16[512,1024]{1,0:T(8,128)(2,1)}, bf16[512,1024]{1,0:T(8,128)(2,1)}, u32[]{:S(2)}, u32[]{:S(2)}) collective-permute-start(bf16[512,1024]{1,0:T(8,128)(2,1)} %get-tuple-element.20), channel_id=1, source_target_pairs={{0,6},{1,7},{2,0},{3,1},{4,2},{5,3},{6,4},{7,5},{8,14},{9,15},{10,... | collective-permute-start | bytes 3145736 | tf_op jit(solution)/shard_map/ppermute | solution.py:201
  31.9 0.4 slice_reduce_fusion
  32.3 2.0 %gather_fusion = bf16[16,64,1024]{2,1,0:T(8,128)(2,1)} fusion(bf16[12,64,1024]{2,1,0:T(8,128)(2,1)S(1)} %copy-done, s32[1024]{0:T(1024)S(1)} %pad_clamp_fusion), kind=kCustom, calls=%fused_computation | custom fusion | bytes 4194368 | tf_op jit(solution)/shard_map/gather | solution.py:227
  34.3 7.4 %all-to-all-start.1 = ((bf16[16,64,1024]{2,1,0:T(8,128)(2,1)}), bf16[16,64,1024]{2,1,0:T(8,128)(2,1)}, u32[]{:S(2)}, u32[]{:S(2)}) async-start(bf16[16,64,1024]{2,1,0:T(8,128)(2,1)} %gather_fusion), calls=%async_computation.1 | async-start | bytes 4194304 | tf_op jit(solution)/shard_map/all_to_all | solution.py:207
  41.7 2.0 %gather_fusion.1 = bf16[16,64,1024]{2,1,0:T(8,128)(2,1)} fusion(bf16[12,64,1024]{2,1,0:T(8,128)(2,1)S(1)} %copy-done.6, s32[1024]{0:T(1024)S(1)} %pad_clamp_fusion), kind=kCustom, calls=%fused_computation.1 | custom fusion | bytes 4194368 | tf_op jit(solution)/shard_map/gather | solution.py:228
  43.7 10.0 %shard_map.65 = (bf16[512,1024]{1,0:T(8,128)(2,1)}, bf16[512,1024]{1,0:T(8,128)(2,1)}) custom-call(s32[8]{0:T(128)S(1)} %fusion.1.sched, bf16[1024,1024]{1,0:T(8,128)(2,1)} %a_ref.9, bf16[1024,1024]{1,0:T(8,128)(2,1)} %copy-done.5, bf16[1024,8192]{1,0:T(8,128)(2,1)} %w_ref.7, bf16[1024,8192]{1,0:T(8,128)(2,1)} %collective-permute-done.2.wp_ref, ...), custom_call_target="tpu_custom_call" | custom-call | flops 10000000000 | bytes 10000000 | tf_op jit(solution)/shard_map/pallas_call | solution.py:81
  53.8 0.8 collective-permute-start.3
  54.6 2.4 %collective-permute-start.4 = (bf16[512,1024]{1,0:T(8,128)(2,1)}, bf16[512,1024]{1,0:T(8,128)(2,1)}, u32[]{:S(2)}, u32[]{:S(2)}) collective-permute-start(bf16[512,1024]{1,0:T(8,128)(2,1)} %get-tuple-element.19.refs_2_), channel_id=1, source_target_pairs={{0,2},{1,3},{2,4},{3,5},{4,6},{5,7},{6,0},{7,1},{8,10},{9,11},{10,... | collective-permute-start | bytes 3145736 | tf_op jit(solution)/shard_map/ppermute | solution.py:201
  57.0 10.3 %shard_map.66 = (bf16[512,1024]{1,0:T(8,128)(2,1)}, bf16[512,1024]{1,0:T(8,128)(2,1)}) custom-call(s32[8]{0:T(128)S(1)} %fusion.1.sched, bf16[1024,1024]{1,0:T(8,128)(2,1)} %a_ref.9, bf16[1024,1024]{1,0:T(8,128)(2,1)} %copy-done.5, bf16[1024,8192]{1,0:T(8,128)(2,1)} %w_ref.7, bf16[1024,8192]{1,0:T(8,128)(2,1)} %collective-permute-done.2.wp_ref, ...), custom_call_target="tpu_custom_call" | custom-call | flops 10000000000 | bytes 10000000 | tf_op jit(solution)/shard_map/pallas_call | solution.py:81
  67.3 1.0 all-to-all-done.1.refs_0_.refs_1_.refs_2_.refs_3_.refs_4_.refs_5_.refs_6_.refs_7_
  68.3 8.0 %all-to-all-start.2 = ((bf16[16,64,1024]{2,1,0:T(8,128)(2,1)}), bf16[16,64,1024]{2,1,0:T(8,128)(2,1)}, u32[]{:S(2)}, u32[]{:S(2)}) async-start(bf16[16,64,1024]{2,1,0:T(8,128)(2,1)} %gather_fusion.1), calls=%async_computation.2 | async-start | bytes 4194304 | tf_op jit(solution)/shard_map/all_to_all | solution.py:207
  76.3 3.3 %shard_map.68 = bf16[8,64,128]{2,1,0:T(8,128)(2,1)S(1)} custom-call(s32[8]{0:T(128)S(1)} %copy-done.2, bf16[1024,1024]{1,0:T(8,128)(2,1)} %a_ref.9, bf16[16,64,1024]{2,1,0:T(8,128)(2,1)} %all-to-all-done.1.refs_0_.refs_1_.refs_2_.refs_3_.refs_4_.refs_5_.refs_6_.refs_7_, ...), custom_call_target="tpu_custom_call" | custom-call | flops 10000000000 | bytes 10000000 | tf_op jit(solution)/shard_map/pallas_call | solution.py:111
  79.7 1.8 %collective-permute-start.7 = (bf16[512,1024]{1,0:T(8,128)(2,1)S(1)}, bf16[512,1024]{1,0:T(8,128)(2,1)}, u32[]{:S(2)}, u32[]{:S(2)}) collective-permute-start(bf16[512,1024]{1,0:T(8,128)(2,1)S(1)} %copy-done.7), channel_id=1, source_target_pairs={{0,2},{1,3},{2,4},{3,5},{4,6},{5,7},{6,0},{7,1},{8,10},{9,11},{10,... | collective-permute-start | bytes 3145736 | tf_op jit(solution)/shard_map/ppermute | solution.py:201
  81.5 0.3 collective-permute-start.8
  81.9 3.0 %collective-permute-start.10 = (bf16[8,64,128]{2,1,0:T(8,128)(2,1)S(1)}, bf16[8,64,128]{2,1,0:T(8,128)(2,1)S(1)}, u32[]{:S(2)}, u32[]{:S(2)}) collective-permute-start(bf16[8,64,128]{2,1,0:T(8,128)(2,1)S(1)} %add_convert_fusion.refs_4_), channel_id=1, source_target_pairs={{0,2},{1,3},{2,4},{3,5},{4,6},{5,7},{6,0},{7,1},{8,10},{9,11},{10,... | collective-permute-start | bytes 393224 | tf_op jit(solution)/shard_map/ppermute | solution.py:201
  84.9 1.0 collective-permute-start.12
  85.8 10.3 %shard_map.67 = (bf16[512,1024]{1,0:T(8,128)(2,1)}, bf16[512,1024]{1,0:T(8,128)(2,1)}) custom-call(s32[8]{0:T(128)S(1)} %fusion.1.sched, bf16[1024,1024]{1,0:T(8,128)(2,1)} %a_ref.9, bf16[1024,1024]{1,0:T(8,128)(2,1)} %copy-done.5, bf16[1024,8192]{1,0:T(8,128)(2,1)} %w_ref.7, bf16[1024,8192]{1,0:T(8,128)(2,1)} %collective-permute-done.2.wp_ref, ...), custom_call_target="tpu_custom_call" | custom-call | flops 10000000000 | bytes 10000000 | tf_op jit(solution)/shard_map/pallas_call | solution.py:81
  96.2 6.4 %all-to-all-done.2.refs_8_.refs_9_.refs_10_.refs_11_.refs_12_.refs_13_.refs_14_.refs_15_ = bf16[16,64,1024]{2,1,0:T(8,128)(2,1)} async-done(((bf16[16,64,1024]{2,1,0:T(8,128)(2,1)}), bf16[16,64,1024]{2,1,0:T(8,128)(2,1)}, u32[]{:S(2)}, u32[]{:S(2)}) %all-to-all-start.2) | async-done | bytes 2097184 | tf_op jit(solution)/shard_map/all_to_all | solution.py:207
  102.6 6.0 %collective-permute-done.10.refs_5_ = bf16[8,64,128]{2,1,0:T(8,128)(2,1)S(1)} collective-permute-done((bf16[8,64,128]{2,1,0:T(8,128)(2,1)S(1)}, bf16[8,64,128]{2,1,0:T(8,128)(2,1)S(1)}, u32[]{:S(2)}, u32[]{:S(2)}) %collective-permute-start.10) | collective-permute-done | bytes 131104 | tf_op jit(solution)/shard_map/ppermute | solution.py:201
  108.5 1.7 %collective-permute-done.11.refs_6_ = bf16[8,64,128]{2,1,0:T(8,128)(2,1)S(1)} collective-permute-done((bf16[8,64,128]{2,1,0:T(8,128)(2,1)S(1)}, bf16[8,64,128]{2,1,0:T(8,128)(2,1)S(1)}, u32[]{:S(2)}, u32[]{:S(2)}) %collective-permute-start.11) | collective-permute-done | bytes 131104 | tf_op jit(solution)/shard_map/ppermute | solution.py:201
  110.2 3.5 %collective-permute-done.12.refs_7_ = bf16[8,64,128]{2,1,0:T(8,128)(2,1)S(1)} collective-permute-done((bf16[8,64,128]{2,1,0:T(8,128)(2,1)S(1)}, bf16[8,64,128]{2,1,0:T(8,128)(2,1)S(1)}, u32[]{:S(2)}, u32[]{:S(2)}) %collective-permute-start.12) | collective-permute-done | bytes 131104 | tf_op jit(solution)/shard_map/ppermute | solution.py:201
  113.7 0.6 copy-done.13
  114.4 5.7 %shard_map.69 = bf16[1024,1024]{1,0:T(8,128)(2,1)} custom-call(s32[8]{0:T(128)S(1)} %copy-done.2, s32[8]{0:T(128)S(1)} %copy-done.3, bf16[512,1024]{1,0:T(8,128)(2,1)} %get-tuple-element.22.refs_0_, bf16[512,1024]{1,0:T(8,128)(2,1)} %collective-permute-done.7.refs_1_, bf16[512,1024]{1,0:T(8,128)(2,1)} %get-tuple-element.23.refs_2_, ...), custom_call_target="tpu_custom_call" | custom-call | flops 10000000000 | bytes 10000000 | tf_op jit(solution)/shard_map/pallas_call | solution.py:168
  (45 shorter events, 0.8 us)
Async XLA Ops:
  0.0 32.3 %copy-start = (bf16[12,64,1024]{2,1,0:T(8,128)(2,1)S(1)}, bf16[12,64,1024]{2,1,0:T(8,128)(2,1)}, u32[]{:S(2)}) copy-start(bf16[12,64,1024]{2,1,0:T(8,128)(2,1)} %param.8) | copy-start | bytes 4718596
  0.0 2.3 %copy-start.4 = (bf16[1024,1024]{1,0:T(8,128)(2,1)S(1)}, bf16[1024,1024]{1,0:T(8,128)(2,1)}, u32[]{:S(2)}) copy-start(bf16[1024,1024]{1,0:T(8,128)(2,1)} %a_ref.9) | copy-start | bytes 6291460
  0.0 10.6 %copy-start.2 = (s32[8]{0:T(128)S(1)}, s32[8]{0:T(128)}, u32[]{:S(2)}) copy-start(s32[8]{0:T(128)} %adapters.3) | copy-start | bytes 100
  1.9 4.2 %collective-permute-start.1 = (bf16[1024,1024]{1,0:T(8,128)(2,1)S(1)}, bf16[1024,1024]{1,0:T(8,128)(2,1)S(1)}, u32[]{:S(2)}, u32[]{:S(2)}) collective-permute-start(bf16[1024,1024]{1,0:T(8,128)(2,1)S(1)} %constant_dynamic-slice_fusion), channel_id=1, source_target_pairs={{0,1},{1,0},{2,3},{3,2},{4,5},{5,4},{6,7},{7,6},{8,9},{9,8},{10,11... | collective-permute-start | bytes 6291464 | tf_op jit(solution)/shard_map/ppermute | solution.py:204
  2.4 6.8 %collective-permute-start = (bf16[1024,1024]{1,0:T(8,128)(2,1)S(1)}, bf16[1024,1024]{1,0:T(8,128)(2,1)S(1)}, u32[]{:S(2)}, u32[]{:S(2)}) collective-permute-start(bf16[1024,1024]{1,0:T(8,128)(2,1)S(1)} %copy-done.4), channel_id=1, source_target_pairs={{0,1},{1,0},{2,3},{3,2},{4,5},{5,4},{6,7},{7,6},{8,9},{9,8},{10,11... | collective-permute-start | bytes 6291464 | tf_op jit(solution)/shard_map/ppermute | solution.py:204
  6.2 3.0 %copy-start.10 = (bf16[1024,1024]{1,0:T(8,128)(2,1)}, bf16[1024,1024]{1,0:T(8,128)(2,1)S(1)}, u32[]{:S(2)}) copy-start(bf16[1024,1024]{1,0:T(8,128)(2,1)S(1)} %collective-permute-done.1.wp_ref) | copy-start | bytes 6291460
  9.2 1.3 %copy-start.5 = (bf16[1024,1024]{1,0:T(8,128)(2,1)}, bf16[1024,1024]{1,0:T(8,128)(2,1)S(1)}, u32[]{:S(2)}) copy-start(bf16[1024,1024]{1,0:T(8,128)(2,1)S(1)} %collective-permute-done.ap_ref) | copy-start | bytes 6291460
  10.5 33.2 %collective-permute-start.2 = (bf16[1024,8192]{1,0:T(8,128)(2,1)}, bf16[1024,8192]{1,0:T(8,128)(2,1)}, u32[]{:S(2)}, u32[]{:S(2)}) collective-permute-start(bf16[1024,8192]{1,0:T(8,128)(2,1)} %w_ref.7), channel_id=1, source_target_pairs={{0,1},{1,0},{2,3},{3,2},{4,5},{5,4},{6,7},{7,6},{8,9},{9,8},{10,11... | collective-permute-start | bytes 50331656 | tf_op jit(solution)/shard_map/ppermute | solution.py:204
  11.4 20.5 %all-to-all-start = ((s32[16,1,128]{2,1,0:T(1,128)}), s32[16,1,128]{2,1,0:T(1,128)S(1)}, u32[]{:S(2)}, u32[]{:S(2)}) async-start(s32[16,1,128]{2,1,0:T(1,128)} %broadcast_in_dim.16), calls=%async_computation | async-start | bytes 16384 | tf_op jit(solution)/shard_map/all_to_all | solution.py:207
  29.9 27.1 %collective-permute-start.5 = (bf16[512,1024]{1,0:T(8,128)(2,1)}, bf16[512,1024]{1,0:T(8,128)(2,1)}, u32[]{:S(2)}, u32[]{:S(2)}) collective-permute-start(bf16[512,1024]{1,0:T(8,128)(2,1)} %get-tuple-element.17.refs_0_), channel_id=1, source_target_pairs={{0,2},{1,3},{2,4},{3,5},{4,6},{5,7},{6,0},{7,1},{8,10},{9,11},{10,... | collective-permute-start | bytes 3145736 | tf_op jit(solution)/shard_map/ppermute | solution.py:201
  30.4 26.7 %collective-permute-start.6 = (bf16[512,1024]{1,0:T(8,128)(2,1)}, bf16[512,1024]{1,0:T(8,128)(2,1)}, u32[]{:S(2)}, u32[]{:S(2)}) collective-permute-start(bf16[512,1024]{1,0:T(8,128)(2,1)} %get-tuple-element.20), channel_id=1, source_target_pairs={{0,6},{1,7},{2,0},{3,1},{4,2},{5,3},{6,4},{7,5},{8,14},{9,15},{10,... | collective-permute-start | bytes 3145736 | tf_op jit(solution)/shard_map/ppermute | solution.py:201
  34.3 7.4 %copy-start.6 = (bf16[12,64,1024]{2,1,0:T(8,128)(2,1)S(1)}, bf16[12,64,1024]{2,1,0:T(8,128)(2,1)}, u32[]{:S(2)}) copy-start(bf16[12,64,1024]{2,1,0:T(8,128)(2,1)} %param.9) | copy-start | bytes 4718596
  34.3 34.0 %all-to-all-start.1 = ((bf16[16,64,1024]{2,1,0:T(8,128)(2,1)}), bf16[16,64,1024]{2,1,0:T(8,128)(2,1)}, u32[]{:S(2)}, u32[]{:S(2)}) async-start(bf16[16,64,1024]{2,1,0:T(8,128)(2,1)} %gather_fusion), calls=%async_computation.1 | async-start | bytes 4194304 | tf_op jit(solution)/shard_map/all_to_all | solution.py:207
  53.8 31.1 %collective-permute-start.3 = (bf16[512,1024]{1,0:T(8,128)(2,1)}, bf16[512,1024]{1,0:T(8,128)(2,1)S(1)}, u32[]{:S(2)}, u32[]{:S(2)}) collective-permute-start(bf16[512,1024]{1,0:T(8,128)(2,1)} %get-tuple-element.18), channel_id=1, source_target_pairs={{0,6},{1,7},{2,0},{3,1},{4,2},{5,3},{6,4},{7,5},{8,14},{9,15},{10,... | collective-permute-start | bytes 3145736 | tf_op jit(solution)/shard_map/ppermute | solution.py:201
  54.6 30.3 %collective-permute-start.4 = (bf16[512,1024]{1,0:T(8,128)(2,1)}, bf16[512,1024]{1,0:T(8,128)(2,1)}, u32[]{:S(2)}, u32[]{:S(2)}) collective-permute-start(bf16[512,1024]{1,0:T(8,128)(2,1)} %get-tuple-element.19.refs_2_), channel_id=1, source_target_pairs={{0,2},{1,3},{2,4},{3,5},{4,6},{5,7},{6,0},{7,1},{8,10},{9,11},{10,... | collective-permute-start | bytes 3145736 | tf_op jit(solution)/shard_map/ppermute | solution.py:201
  68.3 34.3 %all-to-all-start.2 = ((bf16[16,64,1024]{2,1,0:T(8,128)(2,1)}), bf16[16,64,1024]{2,1,0:T(8,128)(2,1)}, u32[]{:S(2)}, u32[]{:S(2)}) async-start(bf16[16,64,1024]{2,1,0:T(8,128)(2,1)} %gather_fusion.1), calls=%async_computation.2 | async-start | bytes 4194304 | tf_op jit(solution)/shard_map/all_to_all | solution.py:207
  76.3 3.4 %copy-start.7 = (bf16[512,1024]{1,0:T(8,128)(2,1)S(1)}, bf16[512,1024]{1,0:T(8,128)(2,1)}, u32[]{:S(2)}) copy-start(bf16[512,1024]{1,0:T(8,128)(2,1)} %get-tuple-element.21.refs_2_.refs_8_) | copy-start | bytes 3145732
  79.6 2.2 %collective-permute-start.9 = (bf16[8,64,128]{2,1,0:T(8,128)(2,1)S(1)}, bf16[8,64,128]{2,1,0:T(8,128)(2,1)S(1)}, u32[]{:S(2)}, u32[]{:S(2)}) collective-permute-start(bf16[8,64,128]{2,1,0:T(8,128)(2,1)S(1)} %shard_map.68), channel_id=1, source_target_pairs={{0,1},{1,0},{2,3},{3,2},{4,5},{5,4},{6,7},{7,6},{8,9},{9,8},{10,11... | collective-permute-start | bytes 393224 | tf_op jit(solution)/shard_map/ppermute | solution.py:204
  79.7 34.0 %collective-permute-start.7 = (bf16[512,1024]{1,0:T(8,128)(2,1)S(1)}, bf16[512,1024]{1,0:T(8,128)(2,1)}, u32[]{:S(2)}, u32[]{:S(2)}) collective-permute-start(bf16[512,1024]{1,0:T(8,128)(2,1)S(1)} %copy-done.7), channel_id=1, source_target_pairs={{0,2},{1,3},{2,4},{3,5},{4,6},{5,7},{6,0},{7,1},{8,10},{9,11},{10,... | collective-permute-start | bytes 3145736 | tf_op jit(solution)/shard_map/ppermute | solution.py:201
  81.5 32.3 %collective-permute-start.8 = (bf16[512,1024]{1,0:T(8,128)(2,1)}, bf16[512,1024]{1,0:T(8,128)(2,1)}, u32[]{:S(2)}, u32[]{:S(2)}) collective-permute-start(bf16[512,1024]{1,0:T(8,128)(2,1)} %get-tuple-element.24), channel_id=1, source_target_pairs={{0,6},{1,7},{2,0},{3,1},{4,2},{5,3},{6,4},{7,5},{8,14},{9,15},{10,... | collective-permute-start | bytes 3145736 | tf_op jit(solution)/shard_map/ppermute | solution.py:201
  81.8 14.3 %copy-start.9 = (bf16[8,64,128]{2,1,0:T(8,128)(2,1)}, bf16[8,64,128]{2,1,0:T(8,128)(2,1)S(1)}, u32[]{:S(2)}) copy-start(bf16[8,64,128]{2,1,0:T(8,128)(2,1)S(1)} %add_convert_fusion.refs_4_) | copy-start | bytes 393220
  81.8 32.5 %copy-start.3 = (s32[8]{0:T(128)S(1)}, s32[8]{0:T(128)}, u32[]{:S(2)}) copy-start(s32[8]{0:T(128)} %fill.1) | copy-start | bytes 100
  81.9 26.7 %collective-permute-start.10 = (bf16[8,64,128]{2,1,0:T(8,128)(2,1)S(1)}, bf16[8,64,128]{2,1,0:T(8,128)(2,1)S(1)}, u32[]{:S(2)}, u32[]{:S(2)}) collective-permute-start(bf16[8,64,128]{2,1,0:T(8,128)(2,1)S(1)} %add_convert_fusion.refs_4_), channel_id=1, source_target_pairs={{0,2},{1,3},{2,4},{3,5},{4,6},{5,7},{6,0},{7,1},{8,10},{9,11},{10,... | collective-permute-start | bytes 393224 | tf_op jit(solution)/shard_map/ppermute | solution.py:201
  84.8 1.0 copy-start.8
  84.8 25.4 %collective-permute-start.11 = (bf16[8,64,128]{2,1,0:T(8,128)(2,1)S(1)}, bf16[8,64,128]{2,1,0:T(8,128)(2,1)S(1)}, u32[]{:S(2)}, u32[]{:S(2)}) collective-permute-start(bf16[8,64,128]{2,1,0:T(8,128)(2,1)S(1)} %add_convert_fusion.refs_4_), channel_id=1, source_target_pairs={{0,4},{1,5},{2,6},{3,7},{4,0},{5,1},{6,2},{7,3},{8,12},{9,13},{10,... | collective-permute-start | bytes 393224 | tf_op jit(solution)/shard_map/ppermute | solution.py:201
  84.9 28.9 %collective-permute-start.12 = (bf16[8,64,128]{2,1,0:T(8,128)(2,1)S(1)}, bf16[8,64,128]{2,1,0:T(8,128)(2,1)S(1)}, u32[]{:S(2)}, u32[]{:S(2)}) collective-permute-start(bf16[8,64,128]{2,1,0:T(8,128)(2,1)S(1)} %add_convert_fusion.refs_4_), channel_id=1, source_target_pairs={{0,6},{1,7},{2,0},{3,1},{4,2},{5,3},{6,4},{7,5},{8,14},{9,15},{10,... | collective-permute-start | bytes 393224 | tf_op jit(solution)/shard_map/ppermute | solution.py:201
  108.5 5.2 %copy-start.11 = (bf16[8,64,128]{2,1,0:T(8,128)(2,1)}, bf16[8,64,128]{2,1,0:T(8,128)(2,1)S(1)}, u32[]{:S(2)}) copy-start(bf16[8,64,128]{2,1,0:T(8,128)(2,1)S(1)} %collective-permute-done.10.refs_5_) | copy-start | bytes 393220
  110.2 3.5 %copy-start.12 = (bf16[8,64,128]{2,1,0:T(8,128)(2,1)}, bf16[8,64,128]{2,1,0:T(8,128)(2,1)S(1)}, u32[]{:S(2)}) copy-start(bf16[8,64,128]{2,1,0:T(8,128)(2,1)S(1)} %collective-permute-done.11.refs_6_) | copy-start | bytes 393220
  113.7 0.6 copy-start.13
  114.4 5.7 %copy-start.1 = (bf16[12,64,1024]{2,1,0:T(8,128)(2,1)S(1)}, bf16[12,64,1024]{2,1,0:T(8,128)(2,1)}, u32[]{:S(2)}) copy-start(bf16[12,64,1024]{2,1,0:T(8,128)(2,1)} %param.8) | copy-start | bytes 4718596
